TPU v7x, 256 devices: a whole 4x4x8 slice. The times are simulated.
256 devices in a mesh: seq: 8 (over z_lo, core), chan: 8 (over x, z_hi), batch: 4 (over y).
Axes of the slice: x: 4, y: 4, z: 8 (z_hi: 2, z_lo: 4; z = z_hi * 4 + z_lo), core: 2. Of those that a mesh axis runs over, the one named last changes fastest.
Arguments:
- tokens: bfloat16 [262144, 1024], P(('batch', 'seq'), 'chan'), parts along dimension 0, may hold values from -6 to 6
- gate_in: bfloat16 [262144, 1024], P(('batch', 'seq'), 'chan'), parts along dimension 0, may hold values from -6 to 6
- mix_first: bfloat16 [512, 512], replicated, may hold values from -0.25 to 0.25
- mix_second: bfloat16 [128, 128], replicated, may hold values from -0.5 to 0.5
- twiddle: float32 [128, 512], P('seq'), may hold values from 0.5 to 2
- out_proj: bfloat16 [1024, 1024], replicated, may hold values from -0.1875 to 0.1875
Outputs:
- mixed: bfloat16 [262144, 1024], P(('batch', 'seq'), 'chan'), parts along dimension 0
There are 4 independent parts, one for each index of `batch`. A program takes and returns all parts, laid end to end along the dimension named above; an argument that names none is the same for every part. Nothing has to cross between parts.
All inputs are finite; a program needn't handle non-finite values.
Results may differ from a plain program's by a relative error of at most 0.012.
Values may be sent and summed in bfloat16 or wider, within the bound.
A program may use at most 128 MiB of HBM per device.

v0:
```python
import jax
import jax.numpy as jnp
from jax import lax
from jax.sharding import PartitionSpec as P

B1 = 512


def body(tokens, gate_in, mix_first, mix_second, twiddle, out_proj):
    seq_rows, chan_cols = tokens.shape
    blocks_here = seq_rows // B1
    blocked = tokens.reshape(blocks_here, B1, chan_cols)
    first_mixed = jnp.einsum("ik,bkc->bic", mix_first, blocked, preferred_element_type=jnp.float32)
    first_mixed = (first_mixed * twiddle[:, :, None]).astype(jnp.bfloat16)
    second_mixed = jnp.einsum(
        "jb,bic->jic",
        mix_second,
        lax.all_to_all(first_mixed, "seq", split_axis=1, concat_axis=0, tiled=True),
        preferred_element_type=jnp.float32,
    )
    second_mixed = second_mixed.astype(jnp.bfloat16)
    returned = lax.all_to_all(second_mixed, "seq", split_axis=0, concat_axis=1, tiled=True)
    hidden = (
        returned.reshape(seq_rows, chan_cols).astype(jnp.float32) * gate_in.astype(jnp.float32)
    ).astype(jnp.bfloat16)
    chan_count = lax.axis_size("chan")
    full_rows = lax.all_to_all(hidden, "chan", split_axis=0, concat_axis=1, tiled=True)
    running = jnp.zeros((full_rows.shape[0], out_proj.shape[1]), jnp.float32)
    for group in range(chan_count):
        columns = full_rows[:, group * chan_cols : (group + 1) * chan_cols]
        weight_rows = out_proj[group * chan_cols : (group + 1) * chan_cols, :]
        partial_term = jnp.dot(columns, weight_rows, preferred_element_type=jnp.float32).astype(
            jnp.bfloat16
        )
        partial_term = lax.optimization_barrier(partial_term)
        running = running + partial_term.astype(jnp.float32)
    projected = running.astype(jnp.bfloat16)
    return lax.all_to_all(projected, "chan", split_axis=1, concat_axis=0, tiled=True)


def solution(mesh):
    placed = (
        P(("batch", "seq"), "chan"),
        P(("batch", "seq"), "chan"),
        P(),
        P(),
        P("seq", None),
        P(),
    )
    return jax.shard_map(
        body, mesh=mesh, in_specs=placed, out_specs=P(("batch", "seq"), "chan"), check_vma=False
    )
```

profile of v0, /device:TPU:119, one launch (start us, length us, event | category | flops | bytes accessed | tf_op | source)
XLA Modules:
  0.0 249.2 jit_solution(2319047103445896781)
XLA Ops:
  0.0 1.6 copy-done
  1.6 3.7 %fusion.6 = bf16[16,512,128]{1,2,0:T(8,128)(2,1)} fusion(f32[16,512]{1,0:T(8,128)} %param.10, bf16[16,512,128]{2,1,0:T(8,128)(2,1)S(1)} %bitcast.35, bf16[512,512]{1,0:T(8,128)(2,1)} %param.8), kind=kOutput, calls=%fused_computation.18 | convolution fusion | flops 1075838976 | bytes 4751360 | tf_op jit(solution)/shard_map/ik,bkc->bic/dot_general | solution.py:13
  5.3 4.5 %copy.26 = bf16[16,512,128]{2,0,1:T(8,128)(2,1)} copy(bf16[16,512,128]{1,2,0:T(8,128)(2,1)} %fusion.6) | data formatting | bytes 4194304 | tf_op jit(solution)/shard_map/convert_element_type | solution.py:14
  9.8 51.8 %all_to_all.65 = bf16[16,512,128]{2,0,1:T(8,128)(2,1)S(1)} all-to-all(bf16[16,512,128]{2,0,1:T(8,128)(2,1)} %copy.26), channel_id=1, replica_groups=mesh['seq'=8,'chan'=8,'batch'=4] {'seq'}, dimensions={1} | all-to-all | bytes 4194304 | tf_op jit(solution)/shard_map/all_to_all | solution.py:18
  61.6 0.5 copy.28
  62.3 3.8 %convert_bitcast_fusion.1 = bf16[128,64,128]{0,2,1:T(8,128)(2,1)} fusion(bf16[128,64,128]{2,1,0:T(8,128)(2,1)S(1)} %bitcast.46, bf16[128,128]{1,0:T(8,128)(2,1)S(1)} %copy-done.4), kind=kOutput, calls=%fused_computation.9 | convolution fusion | flops 269484032 | bytes 4227072 | tf_op jit(solution)/shard_map/jb,bic->jic/dot_general | solution.py:15
  66.2 4.2 %copy.30 = bf16[128,64,128]{2,1,0:T(8,128)(2,1)} copy(bf16[128,64,128]{0,2,1:T(8,128)(2,1)} %convert_bitcast_fusion.1) | data formatting | bytes 4194304 | tf_op jit(solution)/shard_map/convert_element_type | solution.py:21
  70.3 52.6 %all_to_all.66 = bf16[128,64,128]{2,1,0:T(8,128)(2,1)S(1)} all-to-all(bf16[128,64,128]{2,1,0:T(8,128)(2,1)} %copy.30), channel_id=1, replica_groups=mesh['seq'=8,'chan'=8,'batch'=4] {'seq'}, dimensions={0} | all-to-all | bytes 4194304 | tf_op jit(solution)/shard_map/all_to_all | solution.py:22
  122.9 0.5 convert_bitcast_fusion
  123.7 1.3 copy-done.3
  125.0 0.4 fusion
  125.4 57.3 %all_to_all.67 = bf16[8,1024,128]{2,1,0:T(8,128)(2,1)} all-to-all(bf16[8,1024,128]{2,1,0:T(8,128)(2,1)S(1)} %bitcast.49), channel_id=1, replica_groups=mesh['seq'=8,'chan'=8,'batch'=4] {'chan'}, dimensions={0} | all-to-all | bytes 4194304 | tf_op jit(solution)/shard_map/all_to_all | solution.py:27
  182.6 3.9 %copy.32 = bf16[1024,8,128]{0,2,1:T(8,128)(2,1)} copy(bf16[1024,8,128]{2,0,1:T(8,128)(2,1)} %bitcast.47) | data formatting | bytes 4194304 | tf_op jit(solution)/shard_map/all_to_all | solution.py:27
  186.5 1.9 convolution_convert_fusion
  188.5 1.7 convolution_convert_fusion.1
  190.1 0.7 convolution_convert_fusion.2
  190.9 0.7 convolution_convert_fusion.3
  191.6 0.7 convolution_convert_fusion.4
  192.3 0.7 convolution_convert_fusion.5
  193.1 0.7 convolution_convert_fusion.6
  193.8 0.7 convolution_convert_fusion.7
  194.5 2.2 copy_bitcast_fusion
  196.8 51.1 %all_to_all.68 = bf16[1024,8,128]{2,0,1:T(8,128)(2,1)S(1)} all-to-all(bf16[1024,8,128]{2,0,1:T(8,128)(2,1)S(1)} %copy_bitcast_fusion), channel_id=1, replica_groups=mesh['seq'=8,'chan'=8,'batch'=4] {'chan'}, dimensions={1} | all-to-all | bytes 4194304 | tf_op jit(solution)/shard_map/all_to_all | solution.py:38
  247.9 1.3 copy.43
  (9 shorter events, 0.5 us)
Async XLA Ops:
  0.0 1.6 copy-start
  61.6 0.8 copy-start.4
  123.4 1.6 copy-start.3
  186.5 1.9 copy-start.1
  186.5 3.6 %copy-start.2 = (bf16[1024,1024]{1,0:T(8,128)(2,1)S(1)}, bf16[1024,1024]{1,0:T(8,128)(2,1)}, u32[]{:S(2)}) copy-start(bf16[1024,1024]{1,0:T(8,128)(2,1)} %param.11) | copy-start | bytes 6291460
where the time goes:
time: 253 us; the launch traced here: 249 us
  blocking collectives  213 us (84%)
  local copies, waits for them, and re-layouts  17.8 us (7%)
  matrix products  15.4 us (6%)
  other arithmetic  3.08 us (1%)
    all_to_all x1, blocking collectives, body(): lax.all_to_all(hidden, 'chan', split_axis=0, concat_axis=1, tiled=True)  57.3 us
    all_to_all x1, blocking collectives, body(): lax.all_to_all(second_mixed, 'seq', split_axis=0, concat_axis=1, tiled=True)  52.6 us
    all_to_all x1, blocking collectives, body(): lax.all_to_all(first_mixed, 'seq', split_axis=1, concat_axis=0, tiled=True)  51.8 us
    all_to_all x1, blocking collectives, body(): lax.all_to_all(projected, 'chan', split_axis=1, concat_axis=0, tiled=True)  51.1 us
    dot_general x8, matrix products, body(): jnp.dot(columns, weight_rows, preferred_element_type=jnp.float32)  7.93 us

commit v1 on v0

v1 whole, which is shorter than its diff:
```python
import jax
import jax.numpy as jnp
from jax import lax
from jax.sharding import PartitionSpec as P

B1 = 512


def body(tokens, gate_in, mix_first, mix_second, twiddle, out_proj):
    seq_rows, chan_cols = tokens.shape
    n_seq = lax.axis_size("seq")
    n_chan = lax.axis_size("chan")
    blocks_here = seq_rows // B1
    per_dev_i = B1 // n_seq
    d_out = out_proj.shape[1]

    blocked = tokens.reshape(blocks_here, B1, chan_cols)
    mf = mix_first.reshape(n_seq, per_dev_i, B1)
    tw = twiddle.reshape(blocks_here, n_seq, per_dev_i).transpose(1, 0, 2)
    first = jnp.einsum("dik,bkc->dbic", mf, blocked, preferred_element_type=jnp.float32)
    first = (first * tw[:, :, :, None]).astype(jnp.bfloat16)
    got = lax.all_to_all(first, "seq", split_axis=0, concat_axis=0, tiled=False)
    got = got.reshape(n_seq * blocks_here, per_dev_i * chan_cols)
    second = jnp.dot(mix_second, got, preferred_element_type=jnp.float32).astype(jnp.bfloat16)
    second = second.reshape(n_seq, blocks_here, per_dev_i, chan_cols)
    back = lax.all_to_all(second, "seq", split_axis=0, concat_axis=0, tiled=False)
    back = back.transpose(1, 0, 2, 3).reshape(seq_rows, chan_cols)
    hidden = (back.astype(jnp.float32) * gate_in.astype(jnp.float32)).astype(jnp.bfloat16)
    rows_per = seq_rows // n_chan
    hidden = hidden.reshape(n_chan, rows_per, chan_cols)
    full = lax.all_to_all(hidden, "chan", split_axis=0, concat_axis=0, tiled=False)
    wts = out_proj.reshape(n_chan, chan_cols, n_chan, d_out // n_chan)
    mixed = jnp.einsum("spc,scex->epx", full, wts, preferred_element_type=jnp.float32)
    mixed = mixed.astype(jnp.bfloat16)
    res = lax.all_to_all(mixed, "chan", split_axis=0, concat_axis=0, tiled=False)
    return res.reshape(seq_rows, chan_cols)


def solution(mesh):
    placed = (
        P(("batch", "seq"), "chan"),
        P(("batch", "seq"), "chan"),
        P(),
        P(),
        P("seq", None),
        P(),
    )
    return jax.shard_map(
        body, mesh=mesh, in_specs=placed, out_specs=P(("batch", "seq"), "chan"), check_vma=False
    )
```

time: 253 us -> 239 us (0.945)
  blocking collectives: 213 us -> 155 us
  waiting for transfers between devices: 0 us -> 45.5 us
  starting transfers between devices: 0 us -> 8.14 us
  matrix products: 15.4 us -> 10.9 us
  local copies, waits for them, and re-layouts: 17.8 us -> 14.6 us
    all_to_all x4 -> x3, blocking collectives: 213 us -> 155 us  [the longest x1 51.6 us: body(): got = lax.all_to_all(first, 'seq', split_axis=0, concat_axis=0, tiled=False)]
    all_to_all x0 -> x1, waiting for transfers between devices: none -> 45.5 us  [body(): lax.all_to_all(hidden, 'chan', split_axis=0, concat_axis=0, tiled=False)]
    all_to_all x0 -> x1, starting transfers between devices: none -> 8.14 us  [body(): lax.all_to_all(hidden, 'chan', split_axis=0, concat_axis=0, tiled=False)]
    dot_general x10 -> x3, matrix products: 15.4 us -> 10.9 us  [the longest x1 4.55 us: body(): jnp.einsum('spc,scex->epx', full, wts, preferred_element_type=jnp.float32)]
    unnamed x11 -> x9, local copies, waits for them, and re-layouts: 4.4 us -> 8.95 us
    all_to_all x2 -> x0, local copies, waits for them, and re-layouts: 4.45 us -> none  [the longest x1 3.91 us: body(): lax.all_to_all(hidden, 'chan', split_axis=0, concat_axis=1, tiled=True)]
    convert_element_type x3, local copies, waits for them, and re-layouts: 8.95 us -> 4.64 us  [the longest x1 4.1 us: body(): jnp.dot(mix_second, got, preferred_element_type=jnp.float32)]
  transfers between devices with their start and end apart: 0 -> 1, of which waited for: 0 -> 1; matrix products, arithmetic and copies ran while one was open for 0% -> 2% of each run, Pallas kernels for 0% -> 0%
where the time goes in v1:
time: 239 us; the launch traced here: 236 us
  blocking collectives  155 us (65%)
  waiting for transfers between devices  45.5 us (19%)
  local copies, waits for them, and re-layouts  14.6 us (6%)
  matrix products  10.9 us (5%)
  starting transfers between devices  8.14 us (3%)
    all_to_all x1, blocking collectives, body(): got = lax.all_to_all(first, 'seq', split_axis=0, concat_axis=0, tiled=False)  51.6 us
    all_to_all x1, blocking collectives, body(): lax.all_to_all(second, 'seq', split_axis=0, concat_axis=0, tiled=False)  51.5 us
    all_to_all x1, blocking collectives, body(): lax.all_to_all(mixed, 'chan', split_axis=0, concat_axis=0, tiled=False)  51.4 us
    all_to_all x1, waiting for transfers between devices, body(): lax.all_to_all(hidden, 'chan', split_axis=0, concat_axis=0, tiled=False)  45.5 us
    unnamed x9, local copies, waits for them, and re-layouts  8.95 us
    all_to_all x1, starting transfers between devices, body(): lax.all_to_all(hidden, 'chan', split_axis=0, concat_axis=0, tiled=False)  8.14 us
  transfers between devices with their start and end apart: 1, of which 1 were waited for; matrix products, arithmetic and copies ran while one was open for 2% of the time, Pallas kernels for 0%

profile of v1, /device:TPU:119, one launch (start us, length us, event | category | flops | bytes accessed | tf_op | source)
XLA Modules:
  0.0 235.9 jit_solution(12180915091885737136)
XLA Ops:
  0.0 0.0 copy-start
  0.0 1.0 reshape.30
  1.0 0.6 copy-done
  1.6 2.5 %fusion.2 = bf16[8,16,64,128]{3,2,0,1:T(8,128)(2,1)S(1)} fusion(bf16[16,512,128,1]{2,1,3,0:T(8,128)(2,1)S(1)} %bitcast.49, bf16[8,64,512,1]{2,1,0,3:T(8,128)(2,1)} %bitcast.58, f32[8,16,64]{2,0,1:T(8,128)S(1)} %bitcast.57), kind=kOutput, calls=%fused_computation.6 | convolution fusion | flops 1075838976 | bytes 4751360 | tf_op jit(solution)/shard_map/dik,bkc->dbic/dot_general | solution.py:20
  4.1 0.2 copy.16
  4.4 0.0 copy-start.2
  4.4 51.6 %all_to_all.20 = bf16[8,16,64,128]{3,2,1,0:T(8,128)(2,1)S(1)} all-to-all(bf16[8,16,64,128]{3,2,1,0:T(8,128)(2,1)S(1)} %copy.16), channel_id=1, replica_groups=mesh['seq'=8,'chan'=8,'batch'=4] {'seq'}, dimensions={0} | all-to-all | bytes 4194304 | tf_op jit(solution)/shard_map/all_to_all | solution.py:22
  56.0 0.0 copy-done.2
  56.0 3.8 %fusion = bf16[128,8192]{0,1:T(8,128)(2,1)} fusion(bf16[128,128]{1,0:T(8,128)(2,1)S(1)} %copy-done.2, bf16[16,8,64,128]{3,2,1,0:T(8,128)(2,1)S(1)} %bitcast.50), kind=kOutput, calls=%fused_computation.1 | convolution fusion | flops 269484032 | bytes 4227072 | tf_op jit(solution)/shard_map/dot_general | solution.py:24
  59.8 4.1 %copy.17 = bf16[128,8192]{1,0:T(8,128)(2,1)} copy(bf16[128,8192]{0,1:T(8,128)(2,1)} %fusion) | data formatting | bytes 4194304 | tf_op jit(solution)/shard_map/convert_element_type | solution.py:24
  63.9 2.2 copy.23
  66.1 51.5 %all_to_all.21 = bf16[8,16,64,128]{3,2,1,0:T(8,128)(2,1)S(1)} all-to-all(bf16[8,16,64,128]{3,2,1,0:T(8,128)(2,1)S(1)} %bitcast.52), channel_id=1, replica_groups=mesh['seq'=8,'chan'=8,'batch'=4] {'seq'}, dimensions={0} | all-to-all | bytes 4194304 | tf_op jit(solution)/shard_map/all_to_all | solution.py:26
  117.6 0.5 convert_bitcast_fusion
  118.1 0.0 copy-start.1
  118.1 0.3 copy.18
  118.4 1.3 copy-done.1
  119.7 1.7 fusion.1
  121.4 8.1 %all-to-all-start.2 = ((bf16[8,1024,128]{2,1,0:T(8,128)(2,1)}), bf16[8,1024,128]{2,1,0:T(8,128)(2,1)}, u32[]{:S(2)}, u32[]{:S(2)}) async-start(bf16[8,1024,128]{2,1,0:T(8,128)(2,1)} %bitcast.54), calls=%async_computation.2 | async-start | bytes 4194304 | tf_op jit(solution)/shard_map/all_to_all | solution.py:31
  129.5 3.5 %copy.24 = bf16[128,8,8,128]{3,2,1,0:T(8,128)(2,1)} copy(bf16[128,8,8,128]{3,1,2,0:T(8,128)(2,1)} %bitcast.55) | data formatting | bytes 4194304
  133.1 45.5 %all-to-all-done.2 = bf16[8,1024,128]{2,1,0:T(8,128)(2,1)} async-done(((bf16[8,1024,128]{2,1,0:T(8,128)(2,1)}), bf16[8,1024,128]{2,1,0:T(8,128)(2,1)}, u32[]{:S(2)}, u32[]{:S(2)}) %all-to-all-start.2) | async-done | bytes 2097184 | tf_op jit(solution)/shard_map/all_to_all | solution.py:31
  178.6 4.6 %fusion.7 = bf16[8,1024,128]{2,1,0:T(8,128)(2,1)S(1)} fusion(bf16[8,128,8,128]{3,2,1,0:T(8,128)(2,1)} %bitcast.56, bf16[8,1024,128]{2,1,0:T(8,128)(2,1)} %all-to-all-done.2), kind=kOutput, calls=%fused_computation.12 | convolution fusion | flops 2148532224 | bytes 6291456 | tf_op jit(solution)/shard_map/spc,scex->epx/dot_general | solution.py:33
  183.2 51.4 %all_to_all.22 = bf16[8,1024,128]{2,1,0:T(8,128)(2,1)S(1)} all-to-all(bf16[8,1024,128]{2,1,0:T(8,128)(2,1)S(1)} %fusion.7), channel_id=1, replica_groups=mesh['seq'=8,'chan'=8,'batch'=4] {'chan'}, dimensions={0} | all-to-all | bytes 4194304 | tf_op jit(solution)/shard_map/all_to_all | solution.py:35
  234.6 1.3 copy.34
Async XLA Ops:
  0.0 1.6 copy-start
  4.4 51.7 %copy-start.2 = (bf16[128,128]{1,0:T(8,128)(2,1)S(1)}, bf16[128,128]{1,0:T(8,128)(2,1)}, u32[]{:S(2)}) copy-start(bf16[128,128]{1,0:T(8,128)(2,1)} %param.9) | copy-start | bytes 98308
  118.1 1.6 copy-start.1
  121.4 57.2 %all-to-all-start.2 = ((bf16[8,1024,128]{2,1,0:T(8,128)(2,1)}), bf16[8,1024,128]{2,1,0:T(8,128)(2,1)}, u32[]{:S(2)}, u32[]{:S(2)}) async-start(bf16[8,1024,128]{2,1,0:T(8,128)(2,1)} %bitcast.54), calls=%async_computation.2 | async-start | bytes 4194304 | tf_op jit(solution)/shard_map/all_to_all | solution.py:31

commit v2 on v1

--- a/solution.py
+++ b/solution.py
@@ -1,9 +1,58 @@
+import functools
+
 import jax
 import jax.numpy as jnp
 from jax import lax
 from jax.sharding import PartitionSpec as P
+from jax.experimental import pallas as pl
+from jax.experimental.pallas import tpu as pltpu
 
 B1 = 512
+
+
+def _a2a_kernel(axis, n, x_ref, o_ref, send_sem, recv_sem, loc_sem):
+    me = lax.axis_index(axis)
+    barrier = pltpu.get_barrier_semaphore()
+    for t in range(1, n):
+        pl.semaphore_signal(barrier, inc=1, device_id={axis: (me + t) % n},
+                            device_id_type=pl.DeviceIdType.MESH)
+    pl.semaphore_wait(barrier, n - 1)
+    local = pltpu.make_async_copy(x_ref.at[me], o_ref.at[me], loc_sem)
+    local.start()
+    copies = []
+    for t in range(1, n):
+        dst = (me + t) % n
+        c = pltpu.make_async_remote_copy(
+            src_ref=x_ref.at[dst],
+            dst_ref=o_ref.at[me],
+            send_sem=send_sem.at[t],
+            recv_sem=recv_sem.at[t],
+            device_id={axis: dst},
+            device_id_type=pl.DeviceIdType.MESH,
+        )
+        c.start()
+        copies.append(c)
+    local.wait()
+    for c in copies:
+        c.wait_send()
+    for c in copies:
+        c.wait_recv()
+
+
+def _a2a(x, axis, cid):
+    n = x.shape[0]
+    return pl.pallas_call(
+        functools.partial(_a2a_kernel, axis, n),
+        out_shape=jax.ShapeDtypeStruct(x.shape, x.dtype),
+        in_specs=[pl.BlockSpec(memory_space=pl.ANY)],
+        out_specs=pl.BlockSpec(memory_space=pl.ANY),
+        scratch_shapes=[
+            pltpu.SemaphoreType.DMA((n,)),
+            pltpu.SemaphoreType.DMA((n,)),
+            pltpu.SemaphoreType.DMA,
+        ],
+        compiler_params=pltpu.CompilerParams(collective_id=cid, has_side_effects=True),
+    )(x)
 
 
 def body(tokens, gate_in, mix_first, mix_second, twiddle, out_proj):
@@ -19,20 +68,20 @@
     tw = twiddle.reshape(blocks_here, n_seq, per_dev_i).transpose(1, 0, 2)
     first = jnp.einsum("dik,bkc->dbic", mf, blocked, preferred_element_type=jnp.float32)
     first = (first * tw[:, :, :, None]).astype(jnp.bfloat16)
-    got = lax.all_to_all(first, "seq", split_axis=0, concat_axis=0, tiled=False)
+    got = _a2a(first, "seq", 0)
     got = got.reshape(n_seq * blocks_here, per_dev_i * chan_cols)
     second = jnp.dot(mix_second, got, preferred_element_type=jnp.float32).astype(jnp.bfloat16)
     second = second.reshape(n_seq, blocks_here, per_dev_i, chan_cols)
-    back = lax.all_to_all(second, "seq", split_axis=0, concat_axis=0, tiled=False)
+    back = _a2a(second, "seq", 1)
     back = back.transpose(1, 0, 2, 3).reshape(seq_rows, chan_cols)
     hidden = (back.astype(jnp.float32) * gate_in.astype(jnp.float32)).astype(jnp.bfloat16)
     rows_per = seq_rows // n_chan
     hidden = hidden.reshape(n_chan, rows_per, chan_cols)
-    full = lax.all_to_all(hidden, "chan", split_axis=0, concat_axis=0, tiled=False)
+    full = _a2a(hidden, "chan", 2)
     wts = out_proj.reshape(n_chan, chan_cols, n_chan, d_out // n_chan)
     mixed = jnp.einsum("spc,scex->epx", full, wts, preferred_element_type=jnp.float32)
     mixed = mixed.astype(jnp.bfloat16)
-    res = lax.all_to_all(mixed, "chan", split_axis=0, concat_axis=0, tiled=False)
+    res = _a2a(mixed, "chan", 3)
     return res.reshape(seq_rows, chan_cols)
 
 

time: 239 us -> 242 us (1.013)
  Pallas kernels: 0 us -> 205 us
  blocking collectives: 155 us -> 0 us
  waiting for transfers between devices: 45.5 us -> 0 us
  starting transfers between devices: 8.14 us -> 0 us
    pallas_call x0 -> x4, Pallas kernels: none -> 205 us  [_a2a(): pl.pallas_call(functools.partial(_a2a_kernel, axis, n), out_shape=jax.Sha...]
    all_to_all x3 -> x0, blocking collectives: 155 us -> none  [the longest x1 51.6 us: body(): got = lax.all_to_all(first, 'seq', split_axis=0, concat_axis=0, tiled=False)]
    all_to_all x1 -> x0, waiting for transfers between devices: 45.5 us -> none  [body(): lax.all_to_all(hidden, 'chan', split_axis=0, concat_axis=0, tiled=False)]
    all_to_all x1 -> x0, starting transfers between devices: 8.14 us -> none  [body(): lax.all_to_all(hidden, 'chan', split_axis=0, concat_axis=0, tiled=False)]
    unnamed x9 -> x11, local copies, waits for them, and re-layouts: 8.95 us -> 11.8 us
  transfers between devices with their start and end apart: 1 -> 0, of which waited for: 1 -> 0; matrix products, arithmetic and copies ran while one was open for 2% -> 0% of each run, Pallas kernels for 0% -> 0%
where the time goes in v2:
time: 242 us; the launch traced here: 239 us
  Pallas kernels  205 us (85%)
  local copies, waits for them, and re-layouts  17 us (7%)
  matrix products  12.5 us (5%)
  other arithmetic  3.77 us (2%)
    pallas_call x4, Pallas kernels, _a2a(): pl.pallas_call(functools.partial(_a2a_kernel, axis, n), out_shape=jax.Sha...  205 us
    unnamed x11, local copies, waits for them, and re-layouts  11.8 us
    dot_general x1, matrix products, body(): jnp.dot(mix_second, got, preferred_element_type=jnp.float32)  5.42 us

profile of v2, /device:TPU:119, one launch (start us, length us, event | category | flops | bytes accessed | tf_op | source)
XLA Modules:
  0.0 238.9 jit_solution(18406877272108946284)
XLA Ops:
  0.0 0.0 copy-start
  0.0 1.6 copy-done
  1.6 0.8 reshape.30
  2.4 3.5 %fusion.2.x_ref = bf16[8,16,64,128]{3,2,1,0:T(8,128)(2,1)} fusion(bf16[16,512,128,1]{2,1,0,3:T(8,128)(2,1)S(1)} %bitcast.51, bf16[8,64,512,1]{2,1,3,0:T(8,128)(2,1)} %bitcast.60, f32[8,16,64]{2,1,0:T(8,128)S(1)} %bitcast.59), kind=kOutput, calls=%fused_computation.6 | convolution fusion | flops 1075838976 | bytes 4751360 | tf_op jit(solution)/shard_map/dik,bkc->dbic/dot_general | solution.py:69
  5.9 0.0 copy-start.3
  5.9 49.3 %shard_map.64 = bf16[8,16,64,128]{3,2,1,0:T(8,128)(2,1)} custom-call(bf16[8,16,64,128]{3,2,1,0:T(8,128)(2,1)} %fusion.2.x_ref), custom_call_target="tpu_custom_call" | custom-call | tf_op jit(solution)/shard_map/pallas_call | solution.py:44
  55.3 0.0 copy-done.3
  55.3 5.4 %fusion = bf16[128,8192]{0,1:T(8,128)(2,1)} fusion(bf16[128,128]{1,0:T(8,128)(2,1)S(1)} %copy-done.3, bf16[16,8,64,128]{3,2,1,0:T(8,128)(2,1)} %bitcast.52), kind=kOutput, calls=%fused_computation.1 | convolution fusion | flops 269484032 | bytes 4227072 | tf_op jit(solution)/shard_map/dot_general | solution.py:73
  60.7 4.1 %copy.13 = bf16[128,8192]{1,0:T(8,128)(2,1)} copy(bf16[128,8192]{0,1:T(8,128)(2,1)} %fusion) | data formatting | bytes 4194304 | tf_op jit(solution)/shard_map/convert_element_type | solution.py:73
  64.8 3.5 %copy.20 = bf16[16,8,64,128]{3,2,1,0:T(8,128)(2,1)} copy(bf16[16,8,64,128]{3,1,2,0:T(8,128)(2,1)} %bitcast.53) | data formatting | bytes 4194304
  68.3 48.8 %shard_map.65 = bf16[8,16,64,128]{3,2,1,0:T(8,128)(2,1)} custom-call(bf16[8,16,64,128]{3,2,1,0:T(8,128)(2,1)} %bitcast.54), custom_call_target="tpu_custom_call" | custom-call | tf_op jit(solution)/shard_map/pallas_call | solution.py:44
  117.1 2.0 convert_bitcast_fusion
  119.1 0.0 copy-start.2
  119.1 0.3 copy.14
  119.4 1.3 copy-done.2
  120.7 1.7 fusion.1
  122.4 74.1 %shard_map.66 = bf16[8,1024,128]{2,1,0:T(8,128)(2,1)} custom-call(bf16[8,1024,128]{2,1,0:T(8,128)(2,1)} %bitcast.56), custom_call_target="tpu_custom_call" | custom-call | tf_op jit(solution)/shard_map/pallas_call | solution.py:44
  196.5 0.0 copy-start.1
  196.5 2.4 copy.21
  198.9 0.0 copy-done.1
  198.9 3.6 %fusion.7.x_ref = bf16[8,1024,128]{2,1,0:T(8,128)(2,1)} fusion(bf16[8,128,8,128]{3,2,1,0:T(8,128)(2,1)S(1)} %bitcast.58, bf16[8,1024,128]{2,1,0:T(8,128)(2,1)S(1)} %copy-done.1), kind=kOutput, calls=%fused_computation.12 | convolution fusion | flops 2148532224 | bytes 6291456 | tf_op jit(solution)/shard_map/spc,scex->epx/dot_general | solution.py:82
  202.5 33.3 %shard_map.67 = bf16[8,1024,128]{2,1,0:T(8,128)(2,1)} custom-call(bf16[8,1024,128]{2,1,0:T(8,128)(2,1)} %fusion.7.x_ref), custom_call_target="tpu_custom_call" | custom-call | tf_op jit(solution)/shard_map/pallas_call | solution.py:44
  235.8 3.0 %copy.33 = bf16[8192,128]{1,0:T(8,128)(2,1)} copy(bf16[8192,128]{1,0:T(8,128)(2,1)} %bitcast.55) | data formatting | bytes 4194304
  (1 shorter events, 0.0 us)
Async XLA Ops:
  0.0 1.6 copy-start
  5.9 49.3 %copy-start.3 = (bf16[128,128]{1,0:T(8,128)(2,1)S(1)}, bf16[128,128]{1,0:T(8,128)(2,1)}, u32[]{:S(2)}) copy-start(bf16[128,128]{1,0:T(8,128)(2,1)} %param.9) | copy-start | bytes 98308
  119.1 1.6 copy-start.2
  196.5 2.4 copy-start.1

commit v3 on v2

--- a/solution.py
+++ b/solution.py
@@ -8,6 +8,7 @@
 from jax.experimental.pallas import tpu as pltpu
 
 B1 = 512
+CHUNKS = 4
 
 
 def _a2a_kernel(axis, n, x_ref, o_ref, send_sem, recv_sem, loc_sem):
@@ -55,6 +56,108 @@
     )(x)
 
 
+def _back_gate_send_kernel(k_chunks, second_ref, gate_ref, full_ref, recv_s, gv, hid,
+                           s_send, s_recv, c_send, c_recv, g_sem):
+    n_s, n_j, n_i, _ = second_ref.shape
+    n_c = full_ref.shape[0]
+    jp = n_j // n_c
+    w = n_i // k_chunks
+    me_s = lax.axis_index("seq")
+    me_c = lax.axis_index("chan")
+    mesh_ids = pl.DeviceIdType.MESH
+    barrier = pltpu.get_barrier_semaphore()
+    for t in range(1, n_s):
+        pl.semaphore_signal(barrier, inc=1, device_id={"seq": (me_s + t) % n_s}, device_id_type=mesh_ids)
+    for t in range(1, n_c):
+        pl.semaphore_signal(barrier, inc=1, device_id={"chan": (me_c + t) % n_c}, device_id_type=mesh_ids)
+    pl.semaphore_wait(barrier, (n_s - 1) + (n_c - 1))
+
+    gcopy = pltpu.make_async_copy(gate_ref, gv, g_sem)
+    gcopy.start()
+    seq_copies = []
+    for k in range(k_chunks):
+        isl = pl.ds(k * w, w)
+        row = []
+        for t in range(n_s):
+            if t == 0:
+                c = pltpu.make_async_copy(second_ref.at[me_s, :, isl], recv_s.at[me_s, :, isl], s_recv.at[k, 0])
+            else:
+                dst = (me_s + t) % n_s
+                c = pltpu.make_async_remote_copy(
+                    src_ref=second_ref.at[dst, :, isl],
+                    dst_ref=recv_s.at[me_s, :, isl],
+                    send_sem=s_send.at[k, t],
+                    recv_sem=s_recv.at[k, t],
+                    device_id={"seq": dst},
+                    device_id_type=mesh_ids,
+                )
+            c.start()
+            row.append(c)
+        seq_copies.append(row)
+    gcopy.wait()
+    chan_copies = []
+    for k in range(k_chunks):
+        isl = pl.ds(k * w, w)
+        for t in range(n_s):
+            if t == 0:
+                seq_copies[k][t].wait()
+            else:
+                seq_copies[k][t].wait_recv()
+        for s in range(n_s):
+            prod = recv_s[s, :, isl, :].astype(jnp.float32) * gv[:, s, isl, :].astype(jnp.float32)
+            hid[:, s, isl, :] = prod.astype(hid.dtype)
+        for t in range(n_c):
+            dst = (me_c + t) % n_c
+            src_view = hid.at[pl.ds(dst * jp, jp), :, isl, :]
+            dst_view = full_ref.at[me_c, :, :, isl, :]
+            if t == 0:
+                c = pltpu.make_async_copy(src_view, dst_view, c_recv.at[k, 0])
+            else:
+                c = pltpu.make_async_remote_copy(
+                    src_ref=src_view,
+                    dst_ref=dst_view,
+                    send_sem=c_send.at[k, t],
+                    recv_sem=c_recv.at[k, t],
+                    device_id={"chan": dst},
+                    device_id_type=mesh_ids,
+                )
+            c.start()
+            chan_copies.append((t, c))
+    for row in seq_copies:
+        for c in row[1:]:
+            c.wait_send()
+    for t, c in chan_copies:
+        if t == 0:
+            c.wait()
+        else:
+            c.wait_send()
+    for t, c in chan_copies:
+        if t != 0:
+            c.wait_recv()
+
+
+def _back_gate_send(second, gate, n_c, k_chunks, cid):
+    n_s, n_j, n_i, cols = second.shape
+    jp = n_j // n_c
+    return pl.pallas_call(
+        functools.partial(_back_gate_send_kernel, k_chunks),
+        out_shape=jax.ShapeDtypeStruct((n_c, jp, n_s, n_i, cols), second.dtype),
+        in_specs=[pl.BlockSpec(memory_space=pl.ANY)] * 2,
+        out_specs=pl.BlockSpec(memory_space=pl.ANY),
+        scratch_shapes=[
+            pltpu.VMEM((n_s, n_j, n_i, cols), second.dtype),
+            pltpu.VMEM((n_j, n_s, n_i, cols), second.dtype),
+            pltpu.VMEM((n_j, n_s, n_i, cols), second.dtype),
+            pltpu.SemaphoreType.DMA((k_chunks, n_s)),
+            pltpu.SemaphoreType.DMA((k_chunks, n_s)),
+            pltpu.SemaphoreType.DMA((k_chunks, n_c)),
+            pltpu.SemaphoreType.DMA((k_chunks, n_c)),
+            pltpu.SemaphoreType.DMA,
+        ],
+        compiler_params=pltpu.CompilerParams(collective_id=cid, has_side_effects=True),
+    )(second, gate)
+
+
 def body(tokens, gate_in, mix_first, mix_second, twiddle, out_proj):
     seq_rows, chan_cols = tokens.shape
     n_seq = lax.axis_size("seq")
@@ -72,12 +175,10 @@
     got = got.reshape(n_seq * blocks_here, per_dev_i * chan_cols)
     second = jnp.dot(mix_second, got, preferred_element_type=jnp.float32).astype(jnp.bfloat16)
     second = second.reshape(n_seq, blocks_here, per_dev_i, chan_cols)
-    back = _a2a(second, "seq", 1)
-    back = back.transpose(1, 0, 2, 3).reshape(seq_rows, chan_cols)
-    hidden = (back.astype(jnp.float32) * gate_in.astype(jnp.float32)).astype(jnp.bfloat16)
+    gate = gate_in.reshape(blocks_here, n_seq, per_dev_i, chan_cols)
+    full = _back_gate_send(second, gate, n_chan, CHUNKS, 1)
     rows_per = seq_rows // n_chan
-    hidden = hidden.reshape(n_chan, rows_per, chan_cols)
-    full = _a2a(hidden, "chan", 2)
+    full = full.reshape(n_chan, rows_per, chan_cols)
     wts = out_proj.reshape(n_chan, chan_cols, n_chan, d_out // n_chan)
     mixed = jnp.einsum("spc,scex->epx", full, wts, preferred_element_type=jnp.float32)
     mixed = mixed.astype(jnp.bfloat16)

time: 242 us -> 247 us (1.021)
  the two profiles are of different devices: /device:TPU:119 before, /device:TPU:1 now
where the time goes in v3:
time: 247 us; the launch traced here: 246 us
  Pallas kernels  218 us (88%)
  local copies, waits for them, and re-layouts  15.5 us (6%)
  matrix products  12.5 us (5%)
    pallas_call x1, Pallas kernels, _back_gate_send(): pl.pallas_call(functools.partial(_back_gate_send_kernel, k_chunks), out_s...  124 us
    pallas_call x2, Pallas kernels, _a2a(): pl.pallas_call(functools.partial(_a2a_kernel, axis, n), out_shape=jax.Sha...  94.4 us
    unnamed x9, local copies, waits for them, and re-layouts  10.5 us
    dot_general x1, matrix products, body(): jnp.dot(mix_second, got, preferred_element_type=jnp.float32)  5.42 us

profile of v3, /device:TPU:1, one launch (start us, length us, event | category | flops | bytes accessed | tf_op | source)
XLA Modules:
  0.0 246.5 jit_solution(2414719733613161950)
XLA Ops:
  0.0 0.0 copy-start
  0.0 1.6 copy-done
  1.6 0.8 reshape.30
  2.4 3.5 %fusion.1.x_ref = bf16[8,16,64,128]{3,2,1,0:T(8,128)(2,1)} fusion(bf16[16,512,128,1]{2,1,0,3:T(8,128)(2,1)S(1)} %bitcast.44, bf16[8,64,512,1]{2,1,3,0:T(8,128)(2,1)} %bitcast.54, f32[8,16,64]{2,1,0:T(8,128)S(1)} %bitcast.53), kind=kOutput, calls=%fused_computation.4 | convolution fusion | flops 1075838976 | bytes 4751360 | tf_op jit(solution)/shard_map/dik,bkc->dbic/dot_general | solution.py:172
  5.9 0.0 copy-start.2
  5.9 41.6 %shard_map.64 = bf16[8,16,64,128]{3,2,1,0:T(8,128)(2,1)} custom-call(bf16[8,16,64,128]{3,2,1,0:T(8,128)(2,1)} %fusion.1.x_ref), custom_call_target="tpu_custom_call" | custom-call | tf_op jit(solution)/shard_map/pallas_call | solution.py:45
  47.6 0.0 copy-done.2
  47.6 5.4 %fusion = bf16[128,8192]{0,1:T(8,128)(2,1)} fusion(bf16[128,128]{1,0:T(8,128)(2,1)S(1)} %copy-done.2, bf16[16,8,64,128]{3,2,1,0:T(8,128)(2,1)} %bitcast.45), kind=kOutput, calls=%fused_computation.1 | convolution fusion | flops 269484032 | bytes 4227072 | tf_op jit(solution)/shard_map/dot_general | solution.py:176
  53.0 4.1 %copy.9 = bf16[128,8192]{1,0:T(8,128)(2,1)} copy(bf16[128,8192]{0,1:T(8,128)(2,1)} %fusion) | data formatting | bytes 4194304 | tf_op jit(solution)/shard_map/convert_element_type | solution.py:176
  57.1 3.5 %copy.15 = bf16[16,8,64,128]{3,2,1,0:T(8,128)(2,1)} copy(bf16[16,8,64,128]{3,1,2,0:T(8,128)(2,1)} %bitcast.47) | data formatting | bytes 4194304
  60.6 124.1 %shard_map.65 = bf16[8,2,8,64,128]{4,3,2,1,0:T(8,128)(2,1)} custom-call(bf16[8,16,64,128]{3,2,1,0:T(8,128)(2,1)} %bitcast.46, bf16[16,8,64,128]{3,2,1,0:T(8,128)(2,1)} %bitcast.49), custom_call_target="tpu_custom_call" | custom-call | tf_op jit(solution)/shard_map/pallas_call | solution.py:142
  184.7 0.0 copy-start.1
  184.7 2.4 copy.16
  187.1 0.0 copy-done.1
  187.1 3.6 %fusion.5.x_ref = bf16[8,1024,128]{2,1,0:T(8,128)(2,1)} fusion(bf16[8,1024,128,1]{2,1,0,3:T(8,128)(2,1)S(1)} %bitcast.50, bf16[8,128,8,128]{3,2,1,0:T(8,128)(2,1)S(1)} %bitcast.52), kind=kOutput, calls=%fused_computation.8 | convolution fusion | flops 2148532224 | bytes 6291456 | tf_op jit(solution)/shard_map/spc,scex->epx/dot_general | solution.py:183
  190.7 52.7 %shard_map.66 = bf16[8,1024,128]{2,1,0:T(8,128)(2,1)} custom-call(bf16[8,1024,128]{2,1,0:T(8,128)(2,1)} %fusion.5.x_ref), custom_call_target="tpu_custom_call" | custom-call | tf_op jit(solution)/shard_map/pallas_call | solution.py:45
  243.4 3.0 %copy.28 = bf16[8192,128]{1,0:T(8,128)(2,1)} copy(bf16[8192,128]{1,0:T(8,128)(2,1)} %bitcast.48) | data formatting | bytes 4194304
  (1 shorter events, 0.0 us)
Async XLA Ops:
  0.0 1.6 copy-start
  5.9 41.6 %copy-start.2 = (bf16[128,128]{1,0:T(8,128)(2,1)S(1)}, bf16[128,128]{1,0:T(8,128)(2,1)}, u32[]{:S(2)}) copy-start(bf16[128,128]{1,0:T(8,128)(2,1)} %param.9) | copy-start | bytes 98308
  184.7 2.4 copy-start.1

commit v4 on v3

--- a/solution.py
+++ b/solution.py
@@ -9,6 +9,7 @@
 
 B1 = 512
 CHUNKS = 4
+LEAD = 2
 
 
 def _a2a_kernel(axis, n, x_ref, o_ref, send_sem, recv_sem, loc_sem):
@@ -74,8 +75,7 @@
 
     gcopy = pltpu.make_async_copy(gate_ref, gv, g_sem)
     gcopy.start()
-    seq_copies = []
-    for k in range(k_chunks):
+    def issue_seq(k):
         isl = pl.ds(k * w, w)
         row = []
         for t in range(n_s):
@@ -93,7 +93,9 @@
                 )
             c.start()
             row.append(c)
-        seq_copies.append(row)
+        return row
+
+    seq_copies = [issue_seq(k) for k in range(min(LEAD, k_chunks))]
     gcopy.wait()
     chan_copies = []
     for k in range(k_chunks):
@@ -123,6 +125,8 @@
                 )
             c.start()
             chan_copies.append((t, c))
+        if k + LEAD < k_chunks:
+            seq_copies.append(issue_seq(k + LEAD))
     for row in seq_copies:
         for c in row[1:]:
             c.wait_send()

time: 247 us -> 236 us (0.955)
  the two profiles are of different devices: /device:TPU:1 before, /device:TPU:119 now
where the time goes in v4:
time: 236 us; the launch traced here: 234 us
  Pallas kernels  206 us (87%)
  local copies, waits for them, and re-layouts  15.5 us (7%)
  matrix products  12.5 us (5%)
    pallas_call x1, Pallas kernels, _back_gate_send(): pl.pallas_call(functools.partial(_back_gate_send_kernel, k_chunks), out_s...  112 us
    pallas_call x2, Pallas kernels, _a2a(): pl.pallas_call(functools.partial(_a2a_kernel, axis, n), out_shape=jax.Sha...  93.9 us
    unnamed x9, local copies, waits for them, and re-layouts  10.5 us
    dot_general x1, matrix products, body(): jnp.dot(mix_second, got, preferred_element_type=jnp.float32)  5.42 us

profile of v4, /device:TPU:119, one launch (start us, length us, event | category | flops | bytes accessed | tf_op | source)
XLA Modules:
  0.0 234.2 jit_solution(16720035987839088829)
XLA Ops:
  0.0 0.0 copy-start
  0.0 1.6 copy-done
  1.6 0.8 reshape.30
  2.4 3.5 %fusion.1.x_ref = bf16[8,16,64,128]{3,2,1,0:T(8,128)(2,1)} fusion(bf16[16,512,128,1]{2,1,0,3:T(8,128)(2,1)S(1)} %bitcast.44, bf16[8,64,512,1]{2,1,3,0:T(8,128)(2,1)} %bitcast.54, f32[8,16,64]{2,1,0:T(8,128)S(1)} %bitcast.53), kind=kOutput, calls=%fused_computation.4 | convolution fusion | flops 1075838976 | bytes 4751360 | tf_op jit(solution)/shard_map/dik,bkc->dbic/dot_general | solution.py:176
  5.9 0.0 copy-start.2
  5.9 49.3 %shard_map.64 = bf16[8,16,64,128]{3,2,1,0:T(8,128)(2,1)} custom-call(bf16[8,16,64,128]{3,2,1,0:T(8,128)(2,1)} %fusion.1.x_ref), custom_call_target="tpu_custom_call" | custom-call | tf_op jit(solution)/shard_map/pallas_call | solution.py:46
  55.3 0.0 copy-done.2
  55.3 5.4 %fusion = bf16[128,8192]{0,1:T(8,128)(2,1)} fusion(bf16[128,128]{1,0:T(8,128)(2,1)S(1)} %copy-done.2, bf16[16,8,64,128]{3,2,1,0:T(8,128)(2,1)} %bitcast.45), kind=kOutput, calls=%fused_computation.1 | convolution fusion | flops 269484032 | bytes 4227072 | tf_op jit(solution)/shard_map/dot_general | solution.py:180
  60.7 4.1 %copy.9 = bf16[128,8192]{1,0:T(8,128)(2,1)} copy(bf16[128,8192]{0,1:T(8,128)(2,1)} %fusion) | data formatting | bytes 4194304 | tf_op jit(solution)/shard_map/convert_element_type | solution.py:180
  64.8 3.5 %copy.15 = bf16[16,8,64,128]{3,2,1,0:T(8,128)(2,1)} copy(bf16[16,8,64,128]{3,1,2,0:T(8,128)(2,1)} %bitcast.47) | data formatting | bytes 4194304
  68.4 112.2 %shard_map.65 = bf16[8,2,8,64,128]{4,3,2,1,0:T(8,128)(2,1)} custom-call(bf16[8,16,64,128]{3,2,1,0:T(8,128)(2,1)} %bitcast.46, bf16[16,8,64,128]{3,2,1,0:T(8,128)(2,1)} %bitcast.49), custom_call_target="tpu_custom_call" | custom-call | tf_op jit(solution)/shard_map/pallas_call | solution.py:146
  180.6 0.0 copy-start.1
  180.6 2.4 %copy.16 = bf16[128,8,8,128]{3,2,1,0:T(8,128)(2,1)S(1)} copy(bf16[128,8,8,128]{3,1,2,0:T(8,128)(2,1)} %bitcast.51) | data formatting | bytes 4194304
  183.0 0.0 copy-done.1
  183.0 3.6 %fusion.5.x_ref = bf16[8,1024,128]{2,1,0:T(8,128)(2,1)} fusion(bf16[8,1024,128,1]{2,1,0,3:T(8,128)(2,1)S(1)} %bitcast.50, bf16[8,128,8,128]{3,2,1,0:T(8,128)(2,1)S(1)} %bitcast.52), kind=kOutput, calls=%fused_computation.8 | convolution fusion | flops 2148532224 | bytes 6291456 | tf_op jit(solution)/shard_map/spc,scex->epx/dot_general | solution.py:187
  186.6 44.6 %shard_map.66 = bf16[8,1024,128]{2,1,0:T(8,128)(2,1)} custom-call(bf16[8,1024,128]{2,1,0:T(8,128)(2,1)} %fusion.5.x_ref), custom_call_target="tpu_custom_call" | custom-call | tf_op jit(solution)/shard_map/pallas_call | solution.py:46
  231.2 3.0 %copy.28 = bf16[8192,128]{1,0:T(8,128)(2,1)} copy(bf16[8192,128]{1,0:T(8,128)(2,1)} %bitcast.48) | data formatting | bytes 4194304
  (1 shorter events, 0.0 us)
Async XLA Ops:
  0.0 1.6 copy-start
  5.9 49.3 %copy-start.2 = (bf16[128,128]{1,0:T(8,128)(2,1)S(1)}, bf16[128,128]{1,0:T(8,128)(2,1)}, u32[]{:S(2)}) copy-start(bf16[128,128]{1,0:T(8,128)(2,1)} %param.9) | copy-start | bytes 98308
  180.6 2.4 %copy-start.1 = (bf16[8,2,8,64,128]{4,3,2,1,0:T(8,128)(2,1)S(1)}, bf16[8,2,8,64,128]{4,3,2,1,0:T(8,128)(2,1)}, u32[]{:S(2)}) copy-start(bf16[8,2,8,64,128]{4,3,2,1,0:T(8,128)(2,1)} %shard_map.65) | copy-start | bytes 6291460

commit v5 on v4

--- a/solution.py
+++ b/solution.py
@@ -106,7 +106,7 @@
             else:
                 seq_copies[k][t].wait_recv()
         for s in range(n_s):
-            prod = recv_s[s, :, isl, :].astype(jnp.float32) * gv[:, s, isl, :].astype(jnp.float32)
+            prod = recv_s[s, :, isl, :].astype(jnp.float32) * gv[:, pl.ds(s * n_i + k * w, w), :].astype(jnp.float32)
             hid[:, s, isl, :] = prod.astype(hid.dtype)
         for t in range(n_c):
             dst = (me_c + t) % n_c
@@ -150,7 +150,7 @@
         out_specs=pl.BlockSpec(memory_space=pl.ANY),
         scratch_shapes=[
             pltpu.VMEM((n_s, n_j, n_i, cols), second.dtype),
-            pltpu.VMEM((n_j, n_s, n_i, cols), second.dtype),
+            pltpu.VMEM((n_j, n_s * n_i, cols), second.dtype),
             pltpu.VMEM((n_j, n_s, n_i, cols), second.dtype),
             pltpu.SemaphoreType.DMA((k_chunks, n_s)),
             pltpu.SemaphoreType.DMA((k_chunks, n_s)),
@@ -162,6 +162,26 @@
     )(second, gate)
 
 
+def _mix_blocks_kernel(m_ref, x_ref, o_ref):
+    m = m_ref[...]
+    for i in range(x_ref.shape[1]):
+        o_ref[:, i, :] = jnp.dot(m, x_ref[:, i, :], preferred_element_type=jnp.float32).astype(o_ref.dtype)
+
+
+def _mix_blocks(m, x, tile=16):
+    rows, n_i, cols = x.shape
+    return pl.pallas_call(
+        _mix_blocks_kernel,
+        out_shape=jax.ShapeDtypeStruct((m.shape[0], n_i, cols), x.dtype),
+        grid=(n_i // tile,),
+        in_specs=[
+            pl.BlockSpec((m.shape[0], rows), lambda t: (0, 0)),
+            pl.BlockSpec((rows, tile, cols), lambda t: (0, t, 0)),
+        ],
+        out_specs=pl.BlockSpec((m.shape[0], tile, cols), lambda t: (0, t, 0)),
+    )(m, x)
+
+
 def body(tokens, gate_in, mix_first, mix_second, twiddle, out_proj):
     seq_rows, chan_cols = tokens.shape
     n_seq = lax.axis_size("seq")
@@ -176,10 +196,9 @@
     first = jnp.einsum("dik,bkc->dbic", mf, blocked, preferred_element_type=jnp.float32)
     first = (first * tw[:, :, :, None]).astype(jnp.bfloat16)
     got = _a2a(first, "seq", 0)
-    got = got.reshape(n_seq * blocks_here, per_dev_i * chan_cols)
-    second = jnp.dot(mix_second, got, preferred_element_type=jnp.float32).astype(jnp.bfloat16)
-    second = second.reshape(n_seq, blocks_here, per_dev_i, chan_cols)
-    gate = gate_in.reshape(blocks_here, n_seq, per_dev_i, chan_cols)
+    got = got.reshape(n_seq * blocks_here, per_dev_i, chan_cols)
+    second = _mix_blocks(mix_second, got).reshape(n_seq, blocks_here, per_dev_i, chan_cols)
+    gate = gate_in.reshape(blocks_here, B1, chan_cols)
     full = _back_gate_send(second, gate, n_chan, CHUNKS, 1)
     rows_per = seq_rows // n_chan
     full = full.reshape(n_chan, rows_per, chan_cols)

time: 236 us -> 233 us (0.987)
  Pallas kernels: 206 us -> 216 us
  local copies, waits for them, and re-layouts: 15.5 us -> 7.85 us
  matrix products: 12.5 us -> 7.07 us
    pallas_call x0 -> x1, Pallas kernels: none -> 10.1 us  [_mix_blocks(): pl.pallas_call(_mix_blocks_kernel, out_shape=jax.ShapeDtypeStruct((m.shap...]
    dot_general x1 -> x0, matrix products: 5.42 us -> none  [body(): jnp.dot(mix_second, got, preferred_element_type=jnp.float32)]
    convert_element_type x1 -> x0, local copies, waits for them, and re-layouts: 4.14 us -> none  [body(): jnp.dot(mix_second, got, preferred_element_type=jnp.float32)]
    unnamed x9 -> x6, local copies, waits for them, and re-layouts: 10.5 us -> 7 us
where the time goes in v5:
time: 233 us; the launch traced here: 231 us
  Pallas kernels  216 us (93%)
  local copies, waits for them, and re-layouts  7.85 us (3%)
  matrix products  7.07 us (3%)
    pallas_call x1, Pallas kernels, _back_gate_send(): pl.pallas_call(functools.partial(_back_gate_send_kernel, k_chunks), out_s...  112 us
    pallas_call x2, Pallas kernels, _a2a(): pl.pallas_call(functools.partial(_a2a_kernel, axis, n), out_shape=jax.Sha...  94 us
    pallas_call x1, Pallas kernels, _mix_blocks(): pl.pallas_call(_mix_blocks_kernel, out_shape=jax.ShapeDtypeStruct((m.shap...  10.1 us
    unnamed x6, local copies, waits for them, and re-layouts  7 us

profile of v5, /device:TPU:119, one launch (start us, length us, event | category | flops | bytes accessed | tf_op | source)
XLA Modules:
  0.0 231.3 jit_solution(8277229900259041618)
XLA Ops:
  0.0 0.0 copy-start
  0.0 1.6 copy-done
  1.6 0.8 reshape.30
  2.4 3.5 %fusion.x_ref = bf16[8,16,64,128]{3,2,1,0:T(8,128)(2,1)} fusion(bf16[16,512,128,1]{2,1,0,3:T(8,128)(2,1)S(1)} %bitcast.35, bf16[8,64,512,1]{2,1,3,0:T(8,128)(2,1)} %bitcast.44, f32[8,16,64]{2,1,0:T(8,128)S(1)} %bitcast.43), kind=kOutput, calls=%fused_computation.2 | convolution fusion | flops 1075838976 | bytes 4751360 | tf_op jit(solution)/shard_map/dik,bkc->dbic/dot_general | solution.py:196
  5.9 49.3 %shard_map.64 = bf16[8,16,64,128]{3,2,1,0:T(8,128)(2,1)} custom-call(bf16[8,16,64,128]{3,2,1,0:T(8,128)(2,1)} %fusion.x_ref), custom_call_target="tpu_custom_call" | custom-call | tf_op jit(solution)/shard_map/pallas_call | solution.py:46
  55.3 10.1 %shard_map.65 = bf16[128,64,128]{2,1,0:T(8,128)(2,1)} custom-call(bf16[128,128]{1,0:T(8,128)(2,1)} %m_ref.1, bf16[128,64,128]{2,1,0:T(8,128)(2,1)} %bitcast.37), custom_call_target="tpu_custom_call" | custom-call | tf_op jit(solution)/shard_map/pallas_call | solution.py:173
  65.4 112.2 %shard_map.66 = bf16[8,2,8,64,128]{4,3,2,1,0:T(8,128)(2,1)} custom-call(bf16[8,16,64,128]{3,2,1,0:T(8,128)(2,1)} %bitcast.36, bf16[16,512,128]{2,1,0:T(8,128)(2,1)} %bitcast.39), custom_call_target="tpu_custom_call" | custom-call | tf_op jit(solution)/shard_map/pallas_call | solution.py:146
  177.6 0.0 copy-start.1
  177.6 2.4 %copy.13 = bf16[128,8,8,128]{3,2,1,0:T(8,128)(2,1)S(1)} copy(bf16[128,8,8,128]{3,1,2,0:T(8,128)(2,1)} %bitcast.41) | data formatting | bytes 4194304
  180.0 0.0 copy-done.1
  180.0 3.6 %fusion.2.x_ref = bf16[8,1024,128]{2,1,0:T(8,128)(2,1)} fusion(bf16[8,1024,128,1]{2,1,0,3:T(8,128)(2,1)S(1)} %bitcast.40, bf16[8,128,8,128]{3,2,1,0:T(8,128)(2,1)S(1)} %bitcast.42), kind=kOutput, calls=%fused_computation.4 | convolution fusion | flops 2148532224 | bytes 6291456 | tf_op jit(solution)/shard_map/spc,scex->epx/dot_general | solution.py:206
  183.6 44.6 %shard_map.67 = bf16[8,1024,128]{2,1,0:T(8,128)(2,1)} custom-call(bf16[8,1024,128]{2,1,0:T(8,128)(2,1)} %fusion.2.x_ref), custom_call_target="tpu_custom_call" | custom-call | tf_op jit(solution)/shard_map/pallas_call | solution.py:46
  228.2 3.0 %copy.21 = bf16[8192,128]{1,0:T(8,128)(2,1)} copy(bf16[8192,128]{1,0:T(8,128)(2,1)} %bitcast.38) | data formatting | bytes 4194304
  (1 shorter events, 0.0 us)
Async XLA Ops:
  0.0 1.6 copy-start
  177.6 2.4 %copy-start.1 = (bf16[8,2,8,64,128]{4,3,2,1,0:T(8,128)(2,1)S(1)}, bf16[8,2,8,64,128]{4,3,2,1,0:T(8,128)(2,1)}, u32[]{:S(2)}) copy-start(bf16[8,2,8,64,128]{4,3,2,1,0:T(8,128)(2,1)} %shard_map.66) | copy-start | bytes 6291460

commit v6 on v5

--- a/solution.py
+++ b/solution.py
@@ -182,6 +182,62 @@
     )(m, x)
 
 
+def _project_send_kernel(full_ref, w_ref, res_ref, stage, send_sem, recv_sem):
+    n_c, rows, cols = full_ref.shape
+    me = lax.axis_index("chan")
+    mesh_ids = pl.DeviceIdType.MESH
+    barrier = pltpu.get_barrier_semaphore()
+    for t in range(1, n_c):
+        pl.semaphore_signal(barrier, inc=1, device_id={"chan": (me + t) % n_c}, device_id_type=mesh_ids)
+    pl.semaphore_wait(barrier, n_c - 1)
+    copies = []
+    for t in list(range(1, n_c)) + [0]:
+        dst = (me + t) % n_c
+        out_cols = pl.ds(pl.multiple_of(dst * cols, cols), cols)
+        acc = jnp.zeros((rows, cols), jnp.float32)
+        for s in range(n_c):
+            acc += jnp.dot(full_ref[s], w_ref[pl.ds(s * cols, cols), out_cols],
+                           preferred_element_type=jnp.float32)
+        stage[t] = acc.astype(stage.dtype)
+        if t == 0:
+            c = pltpu.make_async_copy(stage.at[t], res_ref.at[me], recv_sem.at[0])
+        else:
+            c = pltpu.make_async_remote_copy(
+                src_ref=stage.at[t],
+                dst_ref=res_ref.at[me],
+                send_sem=send_sem.at[t],
+                recv_sem=recv_sem.at[t],
+                device_id={"chan": dst},
+                device_id_type=mesh_ids,
+            )
+        c.start()
+        copies.append((t, c))
+    for t, c in copies:
+        if t == 0:
+            c.wait()
+        else:
+            c.wait_send()
+    for t, c in copies:
+        if t != 0:
+            c.wait_recv()
+
+
+def _project_send(full, w, cid):
+    n_c, rows, cols = full.shape
+    return pl.pallas_call(
+        _project_send_kernel,
+        out_shape=jax.ShapeDtypeStruct((n_c, rows, cols), full.dtype),
+        in_specs=[pl.BlockSpec(memory_space=pltpu.VMEM)] * 2,
+        out_specs=pl.BlockSpec(memory_space=pl.ANY),
+        scratch_shapes=[
+            pltpu.VMEM((n_c, rows, cols), full.dtype),
+            pltpu.SemaphoreType.DMA((n_c,)),
+            pltpu.SemaphoreType.DMA((n_c,)),
+        ],
+        compiler_params=pltpu.CompilerParams(collective_id=cid, has_side_effects=True),
+    )(full, w)
+
+
 def body(tokens, gate_in, mix_first, mix_second, twiddle, out_proj):
     seq_rows, chan_cols = tokens.shape
     n_seq = lax.axis_size("seq")
@@ -202,10 +258,7 @@
     full = _back_gate_send(second, gate, n_chan, CHUNKS, 1)
     rows_per = seq_rows // n_chan
     full = full.reshape(n_chan, rows_per, chan_cols)
-    wts = out_proj.reshape(n_chan, chan_cols, n_chan, d_out // n_chan)
-    mixed = jnp.einsum("spc,scex->epx", full, wts, preferred_element_type=jnp.float32)
-    mixed = mixed.astype(jnp.bfloat16)
-    res = _a2a(mixed, "chan", 3)
+    res = _project_send(full, out_proj, 3)
     return res.reshape(seq_rows, chan_cols)
 
 

time: 233 us -> 243 us (1.043)
  the two profiles are of different devices: /device:TPU:119 before, /device:TPU:91 now
where the time goes in v6:
time: 243 us; the launch traced here: 242 us
  Pallas kernels  233 us (96%)
  local copies, waits for them, and re-layouts  5.48 us (2%)
  matrix products  3.48 us (1%)
    pallas_call x1, Pallas kernels, _back_gate_send(): pl.pallas_call(functools.partial(_back_gate_send_kernel, k_chunks), out_s...  135 us
    pallas_call x1, Pallas kernels, _a2a(): pl.pallas_call(functools.partial(_a2a_kernel, axis, n), out_shape=jax.Sha...  48 us
    pallas_call x1, Pallas kernels, _project_send(): pl.pallas_call(_project_send_kernel, out_shape=jax.ShapeDtypeStruct((n_c,...  40.6 us
    pallas_call x1, Pallas kernels, _mix_blocks(): pl.pallas_call(_mix_blocks_kernel, out_shape=jax.ShapeDtypeStruct((m.shap...  10.1 us

profile of v6, /device:TPU:91, one launch (start us, length us, event | category | flops | bytes accessed | tf_op | source)
XLA Modules:
  0.0 242.4 jit_solution(17410364433391088810)
XLA Ops:
  0.0 0.0 copy-start
  0.0 1.6 copy-done
  1.6 0.8 reshape.27
  2.4 3.5 %fusion.x_ref = bf16[8,16,64,128]{3,2,1,0:T(8,128)(2,1)} fusion(bf16[16,512,128,1]{2,1,0,3:T(8,128)(2,1)S(1)} %bitcast.22, bf16[8,64,512,1]{2,1,3,0:T(8,128)(2,1)} %bitcast.29, f32[8,16,64]{2,1,0:T(8,128)S(1)} %bitcast.28), kind=kOutput, calls=%fused_computation.1 | convolution fusion | flops 1075838976 | bytes 4751360 | tf_op jit(solution)/shard_map/dik,bkc->dbic/dot_general | solution.py:252
  5.9 48.0 %shard_map.64 = bf16[8,16,64,128]{3,2,1,0:T(8,128)(2,1)} custom-call(bf16[8,16,64,128]{3,2,1,0:T(8,128)(2,1)} %fusion.x_ref), custom_call_target="tpu_custom_call" | custom-call | tf_op jit(solution)/shard_map/pallas_call | solution.py:46
  53.9 10.1 %shard_map.65 = bf16[128,64,128]{2,1,0:T(8,128)(2,1)} custom-call(bf16[128,128]{1,0:T(8,128)(2,1)} %m_ref.1, bf16[128,64,128]{2,1,0:T(8,128)(2,1)} %bitcast.26), custom_call_target="tpu_custom_call" | custom-call | tf_op jit(solution)/shard_map/pallas_call | solution.py:173
  64.0 134.7 %shard_map.66 = bf16[8,2,8,64,128]{4,3,2,1,0:T(8,128)(2,1)} custom-call(bf16[8,16,64,128]{3,2,1,0:T(8,128)(2,1)} %bitcast.24, bf16[16,512,128]{2,1,0:T(8,128)(2,1)} %bitcast.27), custom_call_target="tpu_custom_call" | custom-call | tf_op jit(solution)/shard_map/pallas_call | solution.py:146
  198.7 40.6 %shard_map.67 = bf16[8,1024,128]{2,1,0:T(8,128)(2,1)} custom-call(bf16[8,1024,128]{2,1,0:T(8,128)(2,1)} %bitcast.23, bf16[1024,1024]{1,0:T(8,128)(2,1)} %w_ref.1), custom_call_target="tpu_custom_call" | custom-call | tf_op jit(solution)/shard_map/pallas_call | solution.py:227
  239.3 3.0 %copy.14 = bf16[8192,128]{1,0:T(8,128)(2,1)} copy(bf16[8192,128]{1,0:T(8,128)(2,1)} %bitcast.25) | data formatting | bytes 4194304
  (1 shorter events, 0.0 us)
Async XLA Ops:
  0.0 1.6 copy-start

commit v7 on v4

--- a/solution.py
+++ b/solution.py
@@ -57,9 +57,9 @@
     )(x)
 
 
-def _back_gate_send_kernel(k_chunks, second_ref, gate_ref, full_ref, recv_s, gv, hid,
+def _back_gate_send_kernel(k_chunks, m_ref, got_ref, gate_ref, full_ref, sec, recv_s, gv, hid,
                            s_send, s_recv, c_send, c_recv, g_sem):
-    n_s, n_j, n_i, _ = second_ref.shape
+    n_s, n_j, n_i, _ = sec.shape
     n_c = full_ref.shape[0]
     jp = n_j // n_c
     w = n_i // k_chunks
@@ -77,14 +77,18 @@
     gcopy.start()
     def issue_seq(k):
         isl = pl.ds(k * w, w)
+        m = m_ref[...]
+        for i in range(k * w, (k + 1) * w):
+            part = jnp.dot(m, got_ref[:, i, :], preferred_element_type=jnp.float32)
+            sec[:, :, i, :] = part.astype(sec.dtype).reshape(n_s, n_j, part.shape[-1])
         row = []
         for t in range(n_s):
             if t == 0:
-                c = pltpu.make_async_copy(second_ref.at[me_s, :, isl], recv_s.at[me_s, :, isl], s_recv.at[k, 0])
+                c = pltpu.make_async_copy(sec.at[me_s, :, isl], recv_s.at[me_s, :, isl], s_recv.at[k, 0])
             else:
                 dst = (me_s + t) % n_s
                 c = pltpu.make_async_remote_copy(
-                    src_ref=second_ref.at[dst, :, isl],
+                    src_ref=sec.at[dst, :, isl],
                     dst_ref=recv_s.at[me_s, :, isl],
                     send_sem=s_send.at[k, t],
                     recv_sem=s_recv.at[k, t],
@@ -106,7 +110,7 @@
             else:
                 seq_copies[k][t].wait_recv()
         for s in range(n_s):
-            prod = recv_s[s, :, isl, :].astype(jnp.float32) * gv[:, s, isl, :].astype(jnp.float32)
+            prod = recv_s[s, :, isl, :].astype(jnp.float32) * gv[:, pl.ds(s * n_i + k * w, w), :].astype(jnp.float32)
             hid[:, s, isl, :] = prod.astype(hid.dtype)
         for t in range(n_c):
             dst = (me_c + t) % n_c
@@ -140,18 +144,20 @@
             c.wait_recv()
 
 
-def _back_gate_send(second, gate, n_c, k_chunks, cid):
-    n_s, n_j, n_i, cols = second.shape
+def _back_gate_send(m2, got, gate, n_s, n_c, k_chunks, cid):
+    _, n_i, cols = got.shape
+    n_j = got.shape[0] // n_s
     jp = n_j // n_c
     return pl.pallas_call(
         functools.partial(_back_gate_send_kernel, k_chunks),
-        out_shape=jax.ShapeDtypeStruct((n_c, jp, n_s, n_i, cols), second.dtype),
-        in_specs=[pl.BlockSpec(memory_space=pl.ANY)] * 2,
+        out_shape=jax.ShapeDtypeStruct((n_c, jp, n_s, n_i, cols), got.dtype),
+        in_specs=[pl.BlockSpec(memory_space=pltpu.VMEM)] * 2 + [pl.BlockSpec(memory_space=pl.ANY)],
         out_specs=pl.BlockSpec(memory_space=pl.ANY),
         scratch_shapes=[
-            pltpu.VMEM((n_s, n_j, n_i, cols), second.dtype),
-            pltpu.VMEM((n_j, n_s, n_i, cols), second.dtype),
-            pltpu.VMEM((n_j, n_s, n_i, cols), second.dtype),
+            pltpu.VMEM((n_s, n_j, n_i, cols), got.dtype),
+            pltpu.VMEM((n_s, n_j, n_i, cols), got.dtype),
+            pltpu.VMEM((n_j, n_s * n_i, cols), got.dtype),
+            pltpu.VMEM((n_j, n_s, n_i, cols), got.dtype),
             pltpu.SemaphoreType.DMA((k_chunks, n_s)),
             pltpu.SemaphoreType.DMA((k_chunks, n_s)),
             pltpu.SemaphoreType.DMA((k_chunks, n_c)),
@@ -159,7 +165,7 @@
             pltpu.SemaphoreType.DMA,
         ],
         compiler_params=pltpu.CompilerParams(collective_id=cid, has_side_effects=True),
-    )(second, gate)
+    )(m2, got, gate)
 
 
 def body(tokens, gate_in, mix_first, mix_second, twiddle, out_proj):
@@ -176,11 +182,9 @@
     first = jnp.einsum("dik,bkc->dbic", mf, blocked, preferred_element_type=jnp.float32)
     first = (first * tw[:, :, :, None]).astype(jnp.bfloat16)
     got = _a2a(first, "seq", 0)
-    got = got.reshape(n_seq * blocks_here, per_dev_i * chan_cols)
-    second = jnp.dot(mix_second, got, preferred_element_type=jnp.float32).astype(jnp.bfloat16)
-    second = second.reshape(n_seq, blocks_here, per_dev_i, chan_cols)
-    gate = gate_in.reshape(blocks_here, n_seq, per_dev_i, chan_cols)
-    full = _back_gate_send(second, gate, n_chan, CHUNKS, 1)
+    got = got.reshape(n_seq * blocks_here, per_dev_i, chan_cols)
+    gate = gate_in.reshape(blocks_here, B1, chan_cols)
+    full = _back_gate_send(mix_second, got, gate, n_seq, n_chan, CHUNKS, 1)
     rows_per = seq_rows // n_chan
     full = full.reshape(n_chan, rows_per, chan_cols)
     wts = out_proj.reshape(n_chan, chan_cols, n_chan, d_out // n_chan)

time: 236 us -> 227 us (0.962)
  local copies, waits for them, and re-layouts: 15.5 us -> 7.85 us
  matrix products: 12.5 us -> 7.08 us
  Pallas kernels: 206 us -> 210 us
    dot_general x1 -> x0, matrix products: 5.42 us -> none  [body(): jnp.dot(mix_second, got, preferred_element_type=jnp.float32)]
    convert_element_type x1 -> x0, local copies, waits for them, and re-layouts: 4.14 us -> none  [body(): jnp.dot(mix_second, got, preferred_element_type=jnp.float32)]
    pallas_call x1, Pallas kernels: 112 us -> 116 us  [_back_gate_send(): pl.pallas_call(functools.partial(_back_gate_send_kernel, k_chunks), out_s...]
    unnamed x9 -> x6, local copies, waits for them, and re-layouts: 10.5 us -> 7 us
where the time goes in v7:
time: 227 us; the launch traced here: 225 us
  Pallas kernels  210 us (93%)
  local copies, waits for them, and re-layouts  7.85 us (3%)
  matrix products  7.08 us (3%)
    pallas_call x1, Pallas kernels, _back_gate_send(): pl.pallas_call(functools.partial(_back_gate_send_kernel, k_chunks), out_s...  116 us
    pallas_call x2, Pallas kernels, _a2a(): pl.pallas_call(functools.partial(_a2a_kernel, axis, n), out_shape=jax.Sha...  93.9 us
    unnamed x6, local copies, waits for them, and re-layouts  7 us

profile of v7, /device:TPU:119, one launch (start us, length us, event | category | flops | bytes accessed | tf_op | source)
XLA Modules:
  0.0 225.1 jit_solution(4791676837213699494)
XLA Ops:
  0.0 0.0 copy-start
  0.0 1.6 copy-done
  1.6 0.8 reshape.27
  2.4 3.5 %fusion.x_ref = bf16[8,16,64,128]{3,2,1,0:T(8,128)(2,1)} fusion(bf16[16,512,128,1]{2,1,0,3:T(8,128)(2,1)S(1)} %bitcast.34, bf16[8,64,512,1]{2,1,3,0:T(8,128)(2,1)} %bitcast.42, f32[8,16,64]{2,1,0:T(8,128)S(1)} %bitcast.41), kind=kOutput, calls=%fused_computation.2 | convolution fusion | flops 1075838976 | bytes 4751360 | tf_op jit(solution)/shard_map/dik,bkc->dbic/dot_general | solution.py:182
  5.9 49.3 %shard_map.64 = bf16[8,16,64,128]{3,2,1,0:T(8,128)(2,1)} custom-call(bf16[8,16,64,128]{3,2,1,0:T(8,128)(2,1)} %fusion.x_ref), custom_call_target="tpu_custom_call" | custom-call | tf_op jit(solution)/shard_map/pallas_call | solution.py:46
  55.3 116.2 %shard_map.65 = bf16[8,2,8,64,128]{4,3,2,1,0:T(8,128)(2,1)} custom-call(bf16[128,128]{1,0:T(8,128)(2,1)} %m_ref.1, bf16[128,64,128]{2,1,0:T(8,128)(2,1)} %bitcast.35, bf16[16,512,128]{2,1,0:T(8,128)(2,1)} %bitcast.37), custom_call_target="tpu_custom_call" | custom-call | tf_op jit(solution)/shard_map/pallas_call | solution.py:151
  171.5 0.0 copy-start.1
  171.5 2.4 %copy.13 = bf16[128,8,8,128]{3,2,1,0:T(8,128)(2,1)S(1)} copy(bf16[128,8,8,128]{3,1,2,0:T(8,128)(2,1)} %bitcast.39) | data formatting | bytes 4194304
  173.8 0.0 copy-done.1
  173.8 3.6 %fusion.2.x_ref = bf16[8,1024,128]{2,1,0:T(8,128)(2,1)} fusion(bf16[8,1024,128,1]{2,1,0,3:T(8,128)(2,1)S(1)} %bitcast.38, bf16[8,128,8,128]{3,2,1,0:T(8,128)(2,1)S(1)} %bitcast.40), kind=kOutput, calls=%fused_computation.4 | convolution fusion | flops 2148532224 | bytes 6291456 | tf_op jit(solution)/shard_map/spc,scex->epx/dot_general | solution.py:191
  177.4 44.6 %shard_map.66 = bf16[8,1024,128]{2,1,0:T(8,128)(2,1)} custom-call(bf16[8,1024,128]{2,1,0:T(8,128)(2,1)} %fusion.2.x_ref), custom_call_target="tpu_custom_call" | custom-call | tf_op jit(solution)/shard_map/pallas_call | solution.py:46
  222.1 3.0 %copy.21 = bf16[8192,128]{1,0:T(8,128)(2,1)} copy(bf16[8192,128]{1,0:T(8,128)(2,1)} %bitcast.36) | data formatting | bytes 4194304
  (1 shorter events, 0.0 us)
Async XLA Ops:
  0.0 1.6 copy-start
  171.5 2.4 %copy-start.1 = (bf16[8,2,8,64,128]{4,3,2,1,0:T(8,128)(2,1)S(1)}, bf16[8,2,8,64,128]{4,3,2,1,0:T(8,128)(2,1)}, u32[]{:S(2)}) copy-start(bf16[8,2,8,64,128]{4,3,2,1,0:T(8,128)(2,1)} %shard_map.65) | copy-start | bytes 6291460

commit v8 on v7

--- a/solution.py
+++ b/solution.py
@@ -168,6 +168,84 @@
     )(m2, got, gate)
 
 
+def _first_send_kernel(mf_ref, tok_ref, tw_ref, got_ref, stage, send_sem, recv_sem):
+    n, n_b, n_i, cols = stage.shape
+    me = lax.axis_index("seq")
+    mesh_ids = pl.DeviceIdType.MESH
+    barrier = pltpu.get_barrier_semaphore()
+    for t in range(1, n):
+        pl.semaphore_signal(barrier, inc=1, device_id={"seq": (me + t) % n}, device_id_type=mesh_ids)
+    pl.semaphore_wait(barrier, n - 1)
+    copies = []
+    for t in list(range(1, n)) + [0]:
+        dst = (me + t) % n
+        rows = pl.ds(pl.multiple_of(dst * n_i, n_i), n_i)
+        m = mf_ref[rows, :]
+        for b in range(n_b):
+            part = jnp.dot(m, tok_ref[b], preferred_element_type=jnp.float32)
+            stage[t, b] = (part * tw_ref[rows, pl.ds(b, 1)]).astype(stage.dtype)
+        if t == 0:
+            c = pltpu.make_async_copy(stage.at[t], got_ref.at[me], recv_sem.at[0])
+        else:
+            c = pltpu.make_async_remote_copy(
+                src_ref=stage.at[t],
+                dst_ref=got_ref.at[me],
+                send_sem=send_sem.at[t],
+                recv_sem=recv_sem.at[t],
+                device_id={"seq": dst},
+                device_id_type=mesh_ids,
+            )
+        c.start()
+        copies.append((t, c))
+    for t, c in copies:
+        if t == 0:
+            c.wait()
+        else:
+            c.wait_send()
+    for t, c in copies:
+        if t != 0:
+            c.wait_recv()
+
+
+def _first_send(mix_first, blocked, tw_t, n, cid):
+    n_b, _, cols = blocked.shape
+    n_i = mix_first.shape[0] // n
+    return pl.pallas_call(
+        _first_send_kernel,
+        out_shape=jax.ShapeDtypeStruct((n, n_b, n_i, cols), blocked.dtype),
+        in_specs=[pl.BlockSpec(memory_space=pltpu.VMEM)] * 3,
+        out_specs=pl.BlockSpec(memory_space=pl.ANY),
+        scratch_shapes=[
+            pltpu.VMEM((n, n_b, n_i, cols), blocked.dtype),
+            pltpu.SemaphoreType.DMA((n,)),
+            pltpu.SemaphoreType.DMA((n,)),
+        ],
+        compiler_params=pltpu.CompilerParams(collective_id=cid, has_side_effects=True),
+    )(mix_first, blocked, tw_t)
+
+
+def _project_kernel(full_ref, w_ref, o_ref):
+    n_c, _, cols = full_ref.shape
+    acc = jnp.zeros(o_ref.shape[1:], jnp.float32)
+    for s in range(n_c):
+        acc += jnp.dot(full_ref[s], w_ref[pl.ds(s * cols, cols), :], preferred_element_type=jnp.float32)
+    o_ref[0] = acc.astype(o_ref.dtype)
+
+
+def _project(full, w):
+    n_c, rows, cols = full.shape
+    return pl.pallas_call(
+        _project_kernel,
+        out_shape=jax.ShapeDtypeStruct((w.shape[1] // cols, rows, cols), full.dtype),
+        grid=(w.shape[1] // cols,),
+        in_specs=[
+            pl.BlockSpec((n_c, rows, cols), lambda e: (0, 0, 0)),
+            pl.BlockSpec((w.shape[0], cols), lambda e: (0, e)),
+        ],
+        out_specs=pl.BlockSpec((1, rows, cols), lambda e: (e, 0, 0)),
+    )(full, w)
+
+
 def body(tokens, gate_in, mix_first, mix_second, twiddle, out_proj):
     seq_rows, chan_cols = tokens.shape
     n_seq = lax.axis_size("seq")
@@ -177,19 +255,13 @@
     d_out = out_proj.shape[1]
 
     blocked = tokens.reshape(blocks_here, B1, chan_cols)
-    mf = mix_first.reshape(n_seq, per_dev_i, B1)
-    tw = twiddle.reshape(blocks_here, n_seq, per_dev_i).transpose(1, 0, 2)
-    first = jnp.einsum("dik,bkc->dbic", mf, blocked, preferred_element_type=jnp.float32)
-    first = (first * tw[:, :, :, None]).astype(jnp.bfloat16)
-    got = _a2a(first, "seq", 0)
+    got = _first_send(mix_first, blocked, twiddle.T, n_seq, 0)
     got = got.reshape(n_seq * blocks_here, per_dev_i, chan_cols)
     gate = gate_in.reshape(blocks_here, B1, chan_cols)
     full = _back_gate_send(mix_second, got, gate, n_seq, n_chan, CHUNKS, 1)
     rows_per = seq_rows // n_chan
     full = full.reshape(n_chan, rows_per, chan_cols)
-    wts = out_proj.reshape(n_chan, chan_cols, n_chan, d_out // n_chan)
-    mixed = jnp.einsum("spc,scex->epx", full, wts, preferred_element_type=jnp.float32)
-    mixed = mixed.astype(jnp.bfloat16)
+    mixed = _project(full, out_proj)
     res = _a2a(mixed, "chan", 3)
     return res.reshape(seq_rows, chan_cols)
 

time: 227 us -> 233 us (1.026)
  the two profiles are of different devices: /device:TPU:119 before, /device:TPU:55 now
where the time goes in v8:
time: 233 us
  Pallas kernels  228 us (98%)
  local copies, waits for them, and re-layouts  4.64 us (2%)
    pallas_call x1, Pallas kernels, _back_gate_send(): pl.pallas_call(functools.partial(_back_gate_send_kernel, k_chunks), out_s...  125 us
    pallas_call x1, Pallas kernels, _first_send(): pl.pallas_call(_first_send_kernel, out_shape=jax.ShapeDtypeStruct((n, n_b...  52 us
    pallas_call x1, Pallas kernels, _a2a(): pl.pallas_call(functools.partial(_a2a_kernel, axis, n), out_shape=jax.Sha...  41.7 us
    pallas_call x1, Pallas kernels, _project(): pl.pallas_call(_project_kernel, out_shape=jax.ShapeDtypeStruct((w.shape[1...  9.12 us

profile of v8, /device:TPU:55, one launch (start us, length us, event | category | flops | bytes accessed | tf_op | source)
XLA Modules:
  0.0 232.7 jit_solution(6213505323552362548)
XLA Ops:
  0.0 1.6 copy.7
  1.6 52.0 %shard_map.64 = bf16[8,16,64,128]{3,2,1,0:T(8,128)(2,1)} custom-call(bf16[512,512]{1,0:T(8,128)(2,1)} %mf_ref.1, bf16[16,512,128]{2,1,0:T(8,128)(2,1)} %bitcast.10, f32[512,16]{1,0:T(8,128)} %bitcast.11), custom_call_target="tpu_custom_call" | custom-call | tf_op jit(solution)/shard_map/pallas_call | solution.py:213
  53.6 125.2 %shard_map.65 = bf16[8,2,8,64,128]{4,3,2,1,0:T(8,128)(2,1)} custom-call(bf16[128,128]{1,0:T(8,128)(2,1)} %m_ref.1, bf16[128,64,128]{2,1,0:T(8,128)(2,1)} %bitcast.7, bf16[16,512,128]{2,1,0:T(8,128)(2,1)} %bitcast.9), custom_call_target="tpu_custom_call" | custom-call | tf_op jit(solution)/shard_map/pallas_call | solution.py:151
  178.8 9.1 %shard_map.66.x_ref = bf16[8,1024,128]{2,1,0:T(8,128)(2,1)} custom-call(bf16[8,1024,128]{2,1,0:T(8,128)(2,1)} %bitcast.6, bf16[1024,1024]{1,0:T(8,128)(2,1)} %w_ref.1), custom_call_target="tpu_custom_call" | custom-call | tf_op jit(solution)/shard_map/pallas_call | solution.py:237
  188.0 41.7 %shard_map.67 = bf16[8,1024,128]{2,1,0:T(8,128)(2,1)} custom-call(bf16[8,1024,128]{2,1,0:T(8,128)(2,1)} %shard_map.66.x_ref), custom_call_target="tpu_custom_call" | custom-call | tf_op jit(solution)/shard_map/pallas_call | solution.py:46
  229.6 3.0 %copy.9 = bf16[8192,128]{1,0:T(8,128)(2,1)} copy(bf16[8192,128]{1,0:T(8,128)(2,1)} %bitcast.8) | data formatting | bytes 4194304

commit v9 on v8

--- a/solution.py
+++ b/solution.py
@@ -224,28 +224,6 @@
     )(mix_first, blocked, tw_t)
 
 
-def _project_kernel(full_ref, w_ref, o_ref):
-    n_c, _, cols = full_ref.shape
-    acc = jnp.zeros(o_ref.shape[1:], jnp.float32)
-    for s in range(n_c):
-        acc += jnp.dot(full_ref[s], w_ref[pl.ds(s * cols, cols), :], preferred_element_type=jnp.float32)
-    o_ref[0] = acc.astype(o_ref.dtype)
-
-
-def _project(full, w):
-    n_c, rows, cols = full.shape
-    return pl.pallas_call(
-        _project_kernel,
-        out_shape=jax.ShapeDtypeStruct((w.shape[1] // cols, rows, cols), full.dtype),
-        grid=(w.shape[1] // cols,),
-        in_specs=[
-            pl.BlockSpec((n_c, rows, cols), lambda e: (0, 0, 0)),
-            pl.BlockSpec((w.shape[0], cols), lambda e: (0, e)),
-        ],
-        out_specs=pl.BlockSpec((1, rows, cols), lambda e: (e, 0, 0)),
-    )(full, w)
-
-
 def body(tokens, gate_in, mix_first, mix_second, twiddle, out_proj):
     seq_rows, chan_cols = tokens.shape
     n_seq = lax.axis_size("seq")
@@ -261,7 +239,9 @@
     full = _back_gate_send(mix_second, got, gate, n_seq, n_chan, CHUNKS, 1)
     rows_per = seq_rows // n_chan
     full = full.reshape(n_chan, rows_per, chan_cols)
-    mixed = _project(full, out_proj)
+    wts = out_proj.reshape(n_chan, chan_cols, n_chan, d_out // n_chan)
+    mixed = jnp.einsum("spc,scex->epx", full, wts, preferred_element_type=jnp.float32)
+    mixed = mixed.astype(jnp.bfloat16)
     res = _a2a(mixed, "chan", 3)
     return res.reshape(seq_rows, chan_cols)
 

time: 233 us -> 230 us (0.987)
  the two profiles are of different devices: /device:TPU:55 before, /device:TPU:119 now
where the time goes in v9:
time: 230 us
  Pallas kernels  220 us (96%)
  local copies, waits for them, and re-layouts  6.22 us (3%)
  matrix products  3.57 us (2%)
    pallas_call x1, Pallas kernels, _back_gate_send(): pl.pallas_call(functools.partial(_back_gate_send_kernel, k_chunks), out_s...  119 us
    pallas_call x1, Pallas kernels, _first_send(): pl.pallas_call(_first_send_kernel, out_shape=jax.ShapeDtypeStruct((n, n_b...  51.3 us
    pallas_call x1, Pallas kernels, _a2a(): pl.pallas_call(functools.partial(_a2a_kernel, axis, n), out_shape=jax.Sha...  49.6 us
    unnamed x7, local copies, waits for them, and re-layouts  6.22 us

profile of v9, /device:TPU:119, one launch (start us, length us, event | category | flops | bytes accessed | tf_op | source)
XLA Modules:
  0.0 230.0 jit_solution(1669432021790909185)
XLA Ops:
  0.0 1.6 copy.7
  1.6 51.3 %shard_map.64 = bf16[8,16,64,128]{3,2,1,0:T(8,128)(2,1)} custom-call(bf16[512,512]{1,0:T(8,128)(2,1)} %mf_ref.1, bf16[16,512,128]{2,1,0:T(8,128)(2,1)} %bitcast.23, f32[512,16]{1,0:T(8,128)} %bitcast.26), custom_call_target="tpu_custom_call" | custom-call | tf_op jit(solution)/shard_map/pallas_call | solution.py:213
  52.9 0.0 copy-start.1
  52.9 119.3 %shard_map.65 = bf16[8,2,8,64,128]{4,3,2,1,0:T(8,128)(2,1)} custom-call(bf16[128,128]{1,0:T(8,128)(2,1)} %m_ref.1, bf16[128,64,128]{2,1,0:T(8,128)(2,1)} %bitcast.19, bf16[16,512,128]{2,1,0:T(8,128)(2,1)} %bitcast.21), custom_call_target="tpu_custom_call" | custom-call | tf_op jit(solution)/shard_map/pallas_call | solution.py:151
  172.3 0.0 copy-done.1
  172.3 0.0 copy-start
  172.3 0.6 copy.10
  172.9 0.9 copy-done
  173.9 3.6 %fusion.1.x_ref = bf16[8,1024,128]{2,1,0:T(8,128)(2,1)} fusion(bf16[8,1024,128,1]{2,1,0,3:T(8,128)(2,1)S(1)} %bitcast.22, bf16[8,128,8,128]{3,2,1,0:T(8,128)(2,1)S(1)} %bitcast.25), kind=kOutput, calls=%fused_computation.2 | convolution fusion | flops 2148532224 | bytes 6291456 | tf_op jit(solution)/shard_map/spc,scex->epx/dot_general | solution.py:243
  177.4 49.6 %shard_map.66 = bf16[8,1024,128]{2,1,0:T(8,128)(2,1)} custom-call(bf16[8,1024,128]{2,1,0:T(8,128)(2,1)} %fusion.1.x_ref), custom_call_target="tpu_custom_call" | custom-call | tf_op jit(solution)/shard_map/pallas_call | solution.py:46
  227.0 3.0 %copy.16 = bf16[8192,128]{1,0:T(8,128)(2,1)} copy(bf16[8192,128]{1,0:T(8,128)(2,1)} %bitcast.20) | data formatting | bytes 4194304
Async XLA Ops:
  52.9 119.4 %copy-start.1 = (bf16[1024,1024]{1,0:T(8,128)(2,1)S(1)}, bf16[1024,1024]{1,0:T(8,128)(2,1)}, u32[]{:S(2)}) copy-start(bf16[1024,1024]{1,0:T(8,128)(2,1)} %param.11) | copy-start | bytes 6291460
  172.3 1.6 copy-start

commit v10 on v7

--- a/solution.py
+++ b/solution.py
@@ -57,12 +57,13 @@
     )(x)
 
 
-def _back_gate_send_kernel(k_chunks, m_ref, got_ref, gate_ref, full_ref, sec, recv_s, gv, hid,
-                           s_send, s_recv, c_send, c_recv, g_sem):
-    n_s, n_j, n_i, _ = sec.shape
-    n_c = full_ref.shape[0]
+def _layer_tail_kernel(k_chunks, m_ref, got_ref, w_ref, gate_ref, res_ref, sec, recv_s, gv, hid,
+                       fullv, stage, s_send, s_recv, c_send, c_recv, o_send, o_recv, g_sem):
+    n_s, n_j, n_i, cols = sec.shape
+    n_c = fullv.shape[0]
     jp = n_j // n_c
     w = n_i // k_chunks
+    rows = jp * n_s * w
     me_s = lax.axis_index("seq")
     me_c = lax.axis_index("chan")
     mesh_ids = pl.DeviceIdType.MESH
@@ -75,33 +76,59 @@
 
     gcopy = pltpu.make_async_copy(gate_ref, gv, g_sem)
     gcopy.start()
+
+    def exchange(src_view, dst_view, t, dst, axis, send_sem, recv_sem):
+        if t == 0:
+            c = pltpu.make_async_copy(src_view, dst_view, recv_sem)
+        else:
+            c = pltpu.make_async_remote_copy(
+                src_ref=src_view,
+                dst_ref=dst_view,
+                send_sem=send_sem,
+                recv_sem=recv_sem,
+                device_id={axis: dst},
+                device_id_type=mesh_ids,
+            )
+        c.start()
+        return c
+
     def issue_seq(k):
         isl = pl.ds(k * w, w)
         m = m_ref[...]
         for i in range(k * w, (k + 1) * w):
             part = jnp.dot(m, got_ref[:, i, :], preferred_element_type=jnp.float32)
-            sec[:, :, i, :] = part.astype(sec.dtype).reshape(n_s, n_j, part.shape[-1])
+            sec[:, :, i, :] = part.astype(sec.dtype).reshape(n_s, n_j, cols)
         row = []
         for t in range(n_s):
+            dst = (me_s + t) % n_s
+            row.append(exchange(sec.at[dst, :, isl], recv_s.at[me_s, :, isl], t, dst, "seq",
+                                s_send.at[k, t], s_recv.at[k, t]))
+        return row
+
+    def project(k):
+        isl = pl.ds(k * w, w)
+        for t, c in enumerate(chan_copies[k]):
             if t == 0:
-                c = pltpu.make_async_copy(sec.at[me_s, :, isl], recv_s.at[me_s, :, isl], s_recv.at[k, 0])
+                c.wait()
             else:
-                dst = (me_s + t) % n_s
-                c = pltpu.make_async_remote_copy(
-                    src_ref=sec.at[dst, :, isl],
-                    dst_ref=recv_s.at[me_s, :, isl],
-                    send_sem=s_send.at[k, t],
-                    recv_sem=s_recv.at[k, t],
-                    device_id={"seq": dst},
-                    device_id_type=mesh_ids,
-                )
-            c.start()
-            row.append(c)
-        return row
+                c.wait_recv()
+        acc = jnp.zeros((rows, w_ref.shape[1]), jnp.float32)
+        for s in range(n_c):
+            x = fullv[s, :, :, isl, :].reshape(rows, cols)
+            acc += jnp.dot(x, w_ref[pl.ds(s * cols, cols), :], preferred_element_type=jnp.float32)
+        stage[k] = acc.astype(stage.dtype).reshape(jp, n_s, w, w_ref.shape[1])
+        row = []
+        for t in list(range(1, n_c)) + [0]:
+            dst = (me_c + t) % n_c
+            src_view = stage.at[k, :, :, :, pl.ds(pl.multiple_of(dst * cols, cols), cols)]
+            row.append((t, exchange(src_view, res_ref.at[me_c, :, :, isl, :], t, dst, "chan",
+                                    o_send.at[k, t], o_recv.at[k, t])))
+        out_copies.append(row)
 
     seq_copies = [issue_seq(k) for k in range(min(LEAD, k_chunks))]
     gcopy.wait()
     chan_copies = []
+    out_copies = []
     for k in range(k_chunks):
         isl = pl.ds(k * w, w)
         for t in range(n_s):
@@ -112,60 +139,62 @@
         for s in range(n_s):
             prod = recv_s[s, :, isl, :].astype(jnp.float32) * gv[:, pl.ds(s * n_i + k * w, w), :].astype(jnp.float32)
             hid[:, s, isl, :] = prod.astype(hid.dtype)
+        row = []
         for t in range(n_c):
             dst = (me_c + t) % n_c
-            src_view = hid.at[pl.ds(dst * jp, jp), :, isl, :]
-            dst_view = full_ref.at[me_c, :, :, isl, :]
-            if t == 0:
-                c = pltpu.make_async_copy(src_view, dst_view, c_recv.at[k, 0])
-            else:
-                c = pltpu.make_async_remote_copy(
-                    src_ref=src_view,
-                    dst_ref=dst_view,
-                    send_sem=c_send.at[k, t],
-                    recv_sem=c_recv.at[k, t],
-                    device_id={"chan": dst},
-                    device_id_type=mesh_ids,
-                )
-            c.start()
-            chan_copies.append((t, c))
+            row.append(exchange(hid.at[pl.ds(dst * jp, jp), :, isl, :], fullv.at[me_c, :, :, isl, :],
+                                t, dst, "chan", c_send.at[k, t], c_recv.at[k, t]))
+        chan_copies.append(row)
         if k + LEAD < k_chunks:
             seq_copies.append(issue_seq(k + LEAD))
+        if k >= 1:
+            project(k - 1)
+    project(k_chunks - 1)
     for row in seq_copies:
         for c in row[1:]:
             c.wait_send()
-    for t, c in chan_copies:
-        if t == 0:
-            c.wait()
-        else:
+    for row in chan_copies:
+        for c in row[1:]:
             c.wait_send()
-    for t, c in chan_copies:
-        if t != 0:
-            c.wait_recv()
-
-
-def _back_gate_send(m2, got, gate, n_s, n_c, k_chunks, cid):
+    for row in out_copies:
+        for t, c in row:
+            if t == 0:
+                c.wait()
+            else:
+                c.wait_send()
+    for row in out_copies:
+        for t, c in row:
+            if t != 0:
+                c.wait_recv()
+
+
+def _layer_tail(m2, got, w, gate, n_s, n_c, k_chunks, cid):
     _, n_i, cols = got.shape
     n_j = got.shape[0] // n_s
     jp = n_j // n_c
+    dt = got.dtype
     return pl.pallas_call(
-        functools.partial(_back_gate_send_kernel, k_chunks),
-        out_shape=jax.ShapeDtypeStruct((n_c, jp, n_s, n_i, cols), got.dtype),
-        in_specs=[pl.BlockSpec(memory_space=pltpu.VMEM)] * 2 + [pl.BlockSpec(memory_space=pl.ANY)],
+        functools.partial(_layer_tail_kernel, k_chunks),
+        out_shape=jax.ShapeDtypeStruct((n_c, jp, n_s, n_i, cols), dt),
+        in_specs=[pl.BlockSpec(memory_space=pltpu.VMEM)] * 3 + [pl.BlockSpec(memory_space=pl.ANY)],
         out_specs=pl.BlockSpec(memory_space=pl.ANY),
         scratch_shapes=[
-            pltpu.VMEM((n_s, n_j, n_i, cols), got.dtype),
-            pltpu.VMEM((n_s, n_j, n_i, cols), got.dtype),
-            pltpu.VMEM((n_j, n_s * n_i, cols), got.dtype),
-            pltpu.VMEM((n_j, n_s, n_i, cols), got.dtype),
+            pltpu.VMEM((n_s, n_j, n_i, cols), dt),
+            pltpu.VMEM((n_s, n_j, n_i, cols), dt),
+            pltpu.VMEM((n_j, n_s * n_i, cols), dt),
+            pltpu.VMEM((n_j, n_s, n_i, cols), dt),
+            pltpu.VMEM((n_c, jp, n_s, n_i, cols), dt),
+            pltpu.VMEM((k_chunks, jp, n_s, n_i // k_chunks, w.shape[1]), dt),
             pltpu.SemaphoreType.DMA((k_chunks, n_s)),
             pltpu.SemaphoreType.DMA((k_chunks, n_s)),
+            pltpu.SemaphoreType.DMA((k_chunks, n_c)),
+            pltpu.SemaphoreType.DMA((k_chunks, n_c)),
             pltpu.SemaphoreType.DMA((k_chunks, n_c)),
             pltpu.SemaphoreType.DMA((k_chunks, n_c)),
             pltpu.SemaphoreType.DMA,
         ],
         compiler_params=pltpu.CompilerParams(collective_id=cid, has_side_effects=True),
-    )(m2, got, gate)
+    )(m2, got, w, gate)
 
 
 def body(tokens, gate_in, mix_first, mix_second, twiddle, out_proj):
@@ -184,13 +213,7 @@
     got = _a2a(first, "seq", 0)
     got = got.reshape(n_seq * blocks_here, per_dev_i, chan_cols)
     gate = gate_in.reshape(blocks_here, B1, chan_cols)
-    full = _back_gate_send(mix_second, got, gate, n_seq, n_chan, CHUNKS, 1)
-    rows_per = seq_rows // n_chan
-    full = full.reshape(n_chan, rows_per, chan_cols)
-    wts = out_proj.reshape(n_chan, chan_cols, n_chan, d_out // n_chan)
-    mixed = jnp.einsum("spc,scex->epx", full, wts, preferred_element_type=jnp.float32)
-    mixed = mixed.astype(jnp.bfloat16)
-    res = _a2a(mixed, "chan", 3)
+    res = _layer_tail(mix_second, got, out_proj, gate, n_seq, n_chan, CHUNKS, 1)
     return res.reshape(seq_rows, chan_cols)
 
 

time: 227 us -> 254 us (1.12)
  the two profiles are of different devices: /device:TPU:119 before, /device:TPU:41 now
where the time goes in v10:
time: 254 us
  Pallas kernels  245 us (96%)
  local copies, waits for them, and re-layouts  5.48 us (2%)
  matrix products  3.48 us (1%)
    pallas_call x1, Pallas kernels, _layer_tail(): pl.pallas_call(functools.partial(_layer_tail_kernel, k_chunks), out_shape...  195 us
    pallas_call x1, Pallas kernels, _a2a(): pl.pallas_call(functools.partial(_a2a_kernel, axis, n), out_shape=jax.Sha...  50.1 us

profile of v10, /device:TPU:41, one launch (start us, length us, event | category | flops | bytes accessed | tf_op | source)
XLA Modules:
  0.0 253.6 jit_solution(9911999445599458219)
XLA Ops:
  0.0 0.0 copy-start
  0.0 1.6 copy-done
  1.6 0.8 reshape.21
  2.4 3.5 %fusion.x_ref = bf16[8,16,64,128]{3,2,1,0:T(8,128)(2,1)} fusion(bf16[16,512,128,1]{2,1,0,3:T(8,128)(2,1)S(1)} %bitcast.20, bf16[8,64,512,1]{2,1,3,0:T(8,128)(2,1)} %bitcast.25, f32[8,16,64]{2,1,0:T(8,128)S(1)} %bitcast.24), kind=kOutput, calls=%fused_computation.1 | convolution fusion | flops 1075838976 | bytes 4751360 | tf_op jit(solution)/shard_map/dik,bkc->dbic/dot_general | solution.py:211
  5.9 50.1 %shard_map.64 = bf16[8,16,64,128]{3,2,1,0:T(8,128)(2,1)} custom-call(bf16[8,16,64,128]{3,2,1,0:T(8,128)(2,1)} %fusion.x_ref), custom_call_target="tpu_custom_call" | custom-call | tf_op jit(solution)/shard_map/pallas_call | solution.py:46
  56.0 194.5 %shard_map.65 = bf16[8,2,8,64,128]{4,3,2,1,0:T(8,128)(2,1)} custom-call(bf16[128,128]{1,0:T(8,128)(2,1)} %m_ref.1, bf16[128,64,128]{2,1,0:T(8,128)(2,1)} %bitcast.21, bf16[1024,1024]{1,0:T(8,128)(2,1)} %w_ref.1, bf16[16,512,128]{2,1,0:T(8,128)(2,1)} %bitcast.23), custom_call_target="tpu_custom_call" | custom-call | tf_op jit(solution)/shard_map/pallas_call | solution.py:176
  250.5 3.0 %copy.14 = bf16[8192,128]{1,0:T(8,128)(2,1)} copy(bf16[8192,128]{1,0:T(8,128)(2,1)} %bitcast.22) | data formatting | bytes 4194304
  (1 shorter events, 0.0 us)
Async XLA Ops:
  0.0 1.6 copy-start

commit v11 on v7

--- a/solution.py
+++ b/solution.py
@@ -8,7 +8,7 @@
 from jax.experimental.pallas import tpu as pltpu
 
 B1 = 512
-CHUNKS = 4
+CHUNKS = 8
 LEAD = 2
 
 

time: 227 us -> 233 us (1.026)
  the two profiles are of different devices: /device:TPU:119 before, /device:TPU:9 now
where the time goes in v11:
time: 233 us; the launch traced here: 232 us
  Pallas kernels  217 us (93%)
  local copies, waits for them, and re-layouts  7.85 us (3%)
  matrix products  7.09 us (3%)
    pallas_call x1, Pallas kernels, _back_gate_send(): pl.pallas_call(functools.partial(_back_gate_send_kernel, k_chunks), out_s...  124 us
    pallas_call x2, Pallas kernels, _a2a(): pl.pallas_call(functools.partial(_a2a_kernel, axis, n), out_shape=jax.Sha...  93.1 us
    unnamed x6, local copies, waits for them, and re-layouts  7 us

profile of v11, /device:TPU:9, one launch (start us, length us, event | category | flops | bytes accessed | tf_op | source)
XLA Modules:
  0.0 232.4 jit_solution(9870502306437405040)
XLA Ops:
  0.0 0.0 copy-start
  0.0 1.6 copy-done
  1.6 0.8 reshape.27
  2.4 3.5 %fusion.x_ref = bf16[8,16,64,128]{3,2,1,0:T(8,128)(2,1)} fusion(bf16[16,512,128,1]{2,1,0,3:T(8,128)(2,1)S(1)} %bitcast.34, bf16[8,64,512,1]{2,1,3,0:T(8,128)(2,1)} %bitcast.42, f32[8,16,64]{2,1,0:T(8,128)S(1)} %bitcast.41), kind=kOutput, calls=%fused_computation.2 | convolution fusion | flops 1075838976 | bytes 4751360 | tf_op jit(solution)/shard_map/dik,bkc->dbic/dot_general | solution.py:182
  5.9 40.2 %shard_map.64 = bf16[8,16,64,128]{3,2,1,0:T(8,128)(2,1)} custom-call(bf16[8,16,64,128]{3,2,1,0:T(8,128)(2,1)} %fusion.x_ref), custom_call_target="tpu_custom_call" | custom-call | tf_op jit(solution)/shard_map/pallas_call | solution.py:46
  46.2 124.3 %shard_map.65 = bf16[8,2,8,64,128]{4,3,2,1,0:T(8,128)(2,1)} custom-call(bf16[128,128]{1,0:T(8,128)(2,1)} %m_ref.1, bf16[128,64,128]{2,1,0:T(8,128)(2,1)} %bitcast.35, bf16[16,512,128]{2,1,0:T(8,128)(2,1)} %bitcast.37), custom_call_target="tpu_custom_call" | custom-call | tf_op jit(solution)/shard_map/pallas_call | solution.py:151
  170.5 0.0 copy-start.1
  170.5 2.4 %copy.13 = bf16[128,8,8,128]{3,2,1,0:T(8,128)(2,1)S(1)} copy(bf16[128,8,8,128]{3,1,2,0:T(8,128)(2,1)} %bitcast.39) | data formatting | bytes 4194304
  172.9 0.0 copy-done.1
  172.9 3.6 %fusion.2.x_ref = bf16[8,1024,128]{2,1,0:T(8,128)(2,1)} fusion(bf16[8,1024,128,1]{2,1,0,3:T(8,128)(2,1)S(1)} %bitcast.38, bf16[8,128,8,128]{3,2,1,0:T(8,128)(2,1)S(1)} %bitcast.40), kind=kOutput, calls=%fused_computation.4 | convolution fusion | flops 2148532224 | bytes 6291456 | tf_op jit(solution)/shard_map/spc,scex->epx/dot_general | solution.py:191
  176.5 52.9 %shard_map.66 = bf16[8,1024,128]{2,1,0:T(8,128)(2,1)} custom-call(bf16[8,1024,128]{2,1,0:T(8,128)(2,1)} %fusion.2.x_ref), custom_call_target="tpu_custom_call" | custom-call | tf_op jit(solution)/shard_map/pallas_call | solution.py:46
  229.4 3.0 %copy.21 = bf16[8192,128]{1,0:T(8,128)(2,1)} copy(bf16[8192,128]{1,0:T(8,128)(2,1)} %bitcast.36) | data formatting | bytes 4194304
  (1 shorter events, 0.0 us)
Async XLA Ops:
  0.0 1.6 copy-start
  170.5 2.4 %copy-start.1 = (bf16[8,2,8,64,128]{4,3,2,1,0:T(8,128)(2,1)S(1)}, bf16[8,2,8,64,128]{4,3,2,1,0:T(8,128)(2,1)}, u32[]{:S(2)}) copy-start(bf16[8,2,8,64,128]{4,3,2,1,0:T(8,128)(2,1)} %shard_map.65) | copy-start | bytes 6291460

commit v12 on v7

--- a/solution.py
+++ b/solution.py
@@ -9,7 +9,7 @@
 
 B1 = 512
 CHUNKS = 4
-LEAD = 2
+LEAD = 1
 
 
 def _a2a_kernel(axis, n, x_ref, o_ref, send_sem, recv_sem, loc_sem):

time: 227 us -> 229 us (level)
    pallas_call x2, Pallas kernels: 93.9 us -> 103 us  [_a2a(): pl.pallas_call(functools.partial(_a2a_kernel, axis, n), out_shape=jax.Sha...]
    pallas_call x1, Pallas kernels: 116 us -> 110 us  [_back_gate_send(): pl.pallas_call(functools.partial(_back_gate_send_kernel, k_chunks), out_s...]
where the time goes in v12:
time: 229 us; the launch traced here: 227 us
  Pallas kernels  212 us (93%)
  local copies, waits for them, and re-layouts  7.85 us (3%)
  matrix products  7.08 us (3%)
    pallas_call x1, Pallas kernels, _back_gate_send(): pl.pallas_call(functools.partial(_back_gate_send_kernel, k_chunks), out_s...  110 us
    pallas_call x2, Pallas kernels, _a2a(): pl.pallas_call(functools.partial(_a2a_kernel, axis, n), out_shape=jax.Sha...  103 us
    unnamed x6, local copies, waits for them, and re-layouts  7 us

profile of v12, /device:TPU:119, one launch (start us, length us, event | category | flops | bytes accessed | tf_op | source)
XLA Modules:
  0.0 227.5 jit_solution(17491920740284980758)
XLA Ops:
  0.0 0.0 copy-start
  0.0 1.6 copy-done
  1.6 0.8 reshape.27
  2.4 3.5 %fusion.x_ref = bf16[8,16,64,128]{3,2,1,0:T(8,128)(2,1)} fusion(bf16[16,512,128,1]{2,1,0,3:T(8,128)(2,1)S(1)} %bitcast.34, bf16[8,64,512,1]{2,1,3,0:T(8,128)(2,1)} %bitcast.42, f32[8,16,64]{2,1,0:T(8,128)S(1)} %bitcast.41), kind=kOutput, calls=%fused_computation.2 | convolution fusion | flops 1075838976 | bytes 4751360 | tf_op jit(solution)/shard_map/dik,bkc->dbic/dot_general | solution.py:182
  5.9 49.3 %shard_map.64 = bf16[8,16,64,128]{3,2,1,0:T(8,128)(2,1)} custom-call(bf16[8,16,64,128]{3,2,1,0:T(8,128)(2,1)} %fusion.x_ref), custom_call_target="tpu_custom_call" | custom-call | tf_op jit(solution)/shard_map/pallas_call | solution.py:46
  55.3 109.7 %shard_map.65 = bf16[8,2,8,64,128]{4,3,2,1,0:T(8,128)(2,1)} custom-call(bf16[128,128]{1,0:T(8,128)(2,1)} %m_ref.1, bf16[128,64,128]{2,1,0:T(8,128)(2,1)} %bitcast.35, bf16[16,512,128]{2,1,0:T(8,128)(2,1)} %bitcast.37), custom_call_target="tpu_custom_call" | custom-call | tf_op jit(solution)/shard_map/pallas_call | solution.py:151
  164.9 0.0 copy-start.1
  165.0 2.4 %copy.13 = bf16[128,8,8,128]{3,2,1,0:T(8,128)(2,1)S(1)} copy(bf16[128,8,8,128]{3,1,2,0:T(8,128)(2,1)} %bitcast.39) | data formatting | bytes 4194304
  167.3 0.0 copy-done.1
  167.3 3.6 %fusion.2.x_ref = bf16[8,1024,128]{2,1,0:T(8,128)(2,1)} fusion(bf16[8,1024,128,1]{2,1,0,3:T(8,128)(2,1)S(1)} %bitcast.38, bf16[8,128,8,128]{3,2,1,0:T(8,128)(2,1)S(1)} %bitcast.40), kind=kOutput, calls=%fused_computation.4 | convolution fusion | flops 2148532224 | bytes 6291456 | tf_op jit(solution)/shard_map/spc,scex->epx/dot_general | solution.py:191
  170.9 53.5 %shard_map.66 = bf16[8,1024,128]{2,1,0:T(8,128)(2,1)} custom-call(bf16[8,1024,128]{2,1,0:T(8,128)(2,1)} %fusion.2.x_ref), custom_call_target="tpu_custom_call" | custom-call | tf_op jit(solution)/shard_map/pallas_call | solution.py:46
  224.4 3.0 %copy.21 = bf16[8192,128]{1,0:T(8,128)(2,1)} copy(bf16[8192,128]{1,0:T(8,128)(2,1)} %bitcast.36) | data formatting | bytes 4194304
  (1 shorter events, 0.0 us)
Async XLA Ops:
  0.0 1.6 copy-start
  164.9 2.4 %copy-start.1 = (bf16[8,2,8,64,128]{4,3,2,1,0:T(8,128)(2,1)S(1)}, bf16[8,2,8,64,128]{4,3,2,1,0:T(8,128)(2,1)}, u32[]{:S(2)}) copy-start(bf16[8,2,8,64,128]{4,3,2,1,0:T(8,128)(2,1)} %shard_map.65) | copy-start | bytes 6291460

commit v13 on v7

--- a/solution.py
+++ b/solution.py
@@ -14,18 +14,25 @@
 
 def _a2a_kernel(axis, n, x_ref, o_ref, send_sem, recv_sem, loc_sem):
     me = lax.axis_index(axis)
+    cols = o_ref.shape[-1]
+
+    def piece(d):
+        if len(x_ref.shape) == len(o_ref.shape):
+            return x_ref.at[d]
+        return x_ref.at[:, pl.ds(pl.multiple_of(d * cols, cols), cols)]
+
     barrier = pltpu.get_barrier_semaphore()
     for t in range(1, n):
         pl.semaphore_signal(barrier, inc=1, device_id={axis: (me + t) % n},
                             device_id_type=pl.DeviceIdType.MESH)
     pl.semaphore_wait(barrier, n - 1)
-    local = pltpu.make_async_copy(x_ref.at[me], o_ref.at[me], loc_sem)
+    local = pltpu.make_async_copy(piece(me), o_ref.at[me], loc_sem)
     local.start()
     copies = []
     for t in range(1, n):
         dst = (me + t) % n
         c = pltpu.make_async_remote_copy(
-            src_ref=x_ref.at[dst],
+            src_ref=piece(dst),
             dst_ref=o_ref.at[me],
             send_sem=send_sem.at[t],
             recv_sem=recv_sem.at[t],
@@ -41,11 +48,15 @@
         c.wait_recv()
 
 
-def _a2a(x, axis, cid):
-    n = x.shape[0]
+def _a2a(x, axis, cid, n=None):
+    if n is None:
+        n = x.shape[0]
+        shape = x.shape
+    else:
+        shape = (n, x.shape[0], x.shape[1] // n)
     return pl.pallas_call(
         functools.partial(_a2a_kernel, axis, n),
-        out_shape=jax.ShapeDtypeStruct(x.shape, x.dtype),
+        out_shape=jax.ShapeDtypeStruct(shape, x.dtype),
         in_specs=[pl.BlockSpec(memory_space=pl.ANY)],
         out_specs=pl.BlockSpec(memory_space=pl.ANY),
         scratch_shapes=[
@@ -59,8 +70,8 @@
 
 def _back_gate_send_kernel(k_chunks, m_ref, got_ref, gate_ref, full_ref, sec, recv_s, gv, hid,
                            s_send, s_recv, c_send, c_recv, g_sem):
-    n_s, n_j, n_i, _ = sec.shape
-    n_c = full_ref.shape[0]
+    n_s, n_j, n_i, cols = sec.shape
+    n_c = full_ref.shape[-1] // cols
     jp = n_j // n_c
     w = n_i // k_chunks
     me_s = lax.axis_index("seq")
@@ -115,7 +126,7 @@
         for t in range(n_c):
             dst = (me_c + t) % n_c
             src_view = hid.at[pl.ds(dst * jp, jp), :, isl, :]
-            dst_view = full_ref.at[me_c, :, :, isl, :]
+            dst_view = full_ref.at[:, :, isl, pl.ds(pl.multiple_of(me_c * cols, cols), cols)]
             if t == 0:
                 c = pltpu.make_async_copy(src_view, dst_view, c_recv.at[k, 0])
             else:
@@ -150,7 +161,7 @@
     jp = n_j // n_c
     return pl.pallas_call(
         functools.partial(_back_gate_send_kernel, k_chunks),
-        out_shape=jax.ShapeDtypeStruct((n_c, jp, n_s, n_i, cols), got.dtype),
+        out_shape=jax.ShapeDtypeStruct((jp, n_s, n_i, n_c * cols), got.dtype),
         in_specs=[pl.BlockSpec(memory_space=pltpu.VMEM)] * 2 + [pl.BlockSpec(memory_space=pl.ANY)],
         out_specs=pl.BlockSpec(memory_space=pl.ANY),
         scratch_shapes=[
@@ -186,11 +197,9 @@
     gate = gate_in.reshape(blocks_here, B1, chan_cols)
     full = _back_gate_send(mix_second, got, gate, n_seq, n_chan, CHUNKS, 1)
     rows_per = seq_rows // n_chan
-    full = full.reshape(n_chan, rows_per, chan_cols)
-    wts = out_proj.reshape(n_chan, chan_cols, n_chan, d_out // n_chan)
-    mixed = jnp.einsum("spc,scex->epx", full, wts, preferred_element_type=jnp.float32)
-    mixed = mixed.astype(jnp.bfloat16)
-    res = _a2a(mixed, "chan", 3)
+    full = full.reshape(rows_per, n_chan * chan_cols)
+    mixed = jnp.dot(full, out_proj, preferred_element_type=jnp.float32).astype(jnp.bfloat16)
+    res = _a2a(mixed, "chan", 3, n=n_chan)
     return res.reshape(seq_rows, chan_cols)
 
 

time: 227 us -> 227 us (level)
  local copies, waits for them, and re-layouts: 7.85 us -> 5.48 us
  matrix products: 7.08 us -> 9.37 us
    unnamed x6 -> x3, local copies, waits for them, and re-layouts: 7 us -> 4.64 us
    dot_general x1, matrix products: 3.6 us -> 5.87 us  [body(): jnp.dot(full, out_proj, preferred_element_type=jnp.float32)]
where the time goes in v13:
time: 227 us; the launch traced here: 225 us
  Pallas kernels  210 us (93%)
  matrix products  9.37 us (4%)
  local copies, waits for them, and re-layouts  5.48 us (2%)
    pallas_call x1, Pallas kernels, _back_gate_send(): pl.pallas_call(functools.partial(_back_gate_send_kernel, k_chunks), out_s...  116 us
    pallas_call x2, Pallas kernels, _a2a(): pl.pallas_call(functools.partial(_a2a_kernel, axis, n), out_shape=jax.Sha...  93.9 us
    dot_general x1, matrix products, body(): jnp.dot(full, out_proj, preferred_element_type=jnp.float32)  5.87 us
    unnamed x3, local copies, waits for them, and re-layouts  4.64 us

profile of v13, /device:TPU:119, one launch (start us, length us, event | category | flops | bytes accessed | tf_op | source)
XLA Modules:
  0.0 225.0 jit_solution(668959704647426526)
XLA Ops:
  0.0 0.0 copy-start
  0.0 1.6 copy-done
  1.6 0.8 reshape.24
  2.4 3.5 %fusion.x_ref = bf16[8,16,64,128]{3,2,1,0:T(8,128)(2,1)} fusion(bf16[16,512,128,1]{2,1,0,3:T(8,128)(2,1)S(1)} %bitcast.23, bf16[8,64,512,1]{2,1,3,0:T(8,128)(2,1)} %bitcast.29, f32[8,16,64]{2,1,0:T(8,128)S(1)} %bitcast.28), kind=kOutput, calls=%fused_computation.1 | convolution fusion | flops 1075838976 | bytes 4751360 | tf_op jit(solution)/shard_map/dik,bkc->dbic/dot_general | solution.py:193
  5.9 49.3 %shard_map.64 = bf16[8,16,64,128]{3,2,1,0:T(8,128)(2,1)} custom-call(bf16[8,16,64,128]{3,2,1,0:T(8,128)(2,1)} %fusion.x_ref), custom_call_target="tpu_custom_call" | custom-call | tf_op jit(solution)/shard_map/pallas_call | solution.py:57
  55.3 116.2 %shard_map.65 = bf16[2,8,64,1024]{3,2,1,0:T(8,128)(2,1)} custom-call(bf16[128,128]{1,0:T(8,128)(2,1)} %m_ref.1, bf16[128,64,128]{2,1,0:T(8,128)(2,1)} %bitcast.24, bf16[16,512,128]{2,1,0:T(8,128)(2,1)} %bitcast.26), custom_call_target="tpu_custom_call" | custom-call | tf_op jit(solution)/shard_map/pallas_call | solution.py:162
  171.5 5.9 %convolution_convert_fusion.x_ref = bf16[1024,1024]{1,0:T(8,128)(2,1)} fusion(bf16[1024,1024]{1,0:T(8,128)(2,1)} %bitcast.27, bf16[1024,1024]{1,0:T(8,128)(2,1)} %param.11), kind=kOutput, calls=%fused_computation.2 | convolution fusion | flops 2148532224 | bytes 6291456 | tf_op jit(solution)/shard_map/dot_general | solution.py:201
  177.3 44.6 %shard_map.66 = bf16[8,1024,128]{2,1,0:T(8,128)(2,1)} custom-call(bf16[1024,1024]{1,0:T(8,128)(2,1)} %convolution_convert_fusion.x_ref), custom_call_target="tpu_custom_call" | custom-call | tf_op jit(solution)/shard_map/pallas_call | solution.py:57
  222.0 3.0 %copy.14 = bf16[8192,128]{1,0:T(8,128)(2,1)} copy(bf16[8192,128]{1,0:T(8,128)(2,1)} %bitcast.25) | data formatting | bytes 4194304
  (1 shorter events, 0.0 us)
Async XLA Ops:
  0.0 1.6 copy-start

commit v14 on v13

--- a/solution.py
+++ b/solution.py
@@ -179,6 +179,60 @@
     )(m2, got, gate)
 
 
+def _project_send_kernel(full_ref, w_ref, res_ref, stage, send_sem, recv_sem):
+    n_c, rows, cols = stage.shape
+    me = lax.axis_index("chan")
+    mesh_ids = pl.DeviceIdType.MESH
+    barrier = pltpu.get_barrier_semaphore()
+    for t in range(1, n_c):
+        pl.semaphore_signal(barrier, inc=1, device_id={"chan": (me + t) % n_c}, device_id_type=mesh_ids)
+    pl.semaphore_wait(barrier, n_c - 1)
+    copies = []
+    for t in list(range(1, n_c)) + [0]:
+        dst = (me + t) % n_c
+        out_cols = pl.ds(pl.multiple_of(dst * cols, cols), cols)
+        part = jnp.dot(full_ref[...], w_ref[:, out_cols], preferred_element_type=jnp.float32)
+        stage[t] = part.astype(stage.dtype)
+        if t == 0:
+            c = pltpu.make_async_copy(stage.at[t], res_ref.at[me], recv_sem.at[0])
+        else:
+            c = pltpu.make_async_remote_copy(
+                src_ref=stage.at[t],
+                dst_ref=res_ref.at[me],
+                send_sem=send_sem.at[t],
+                recv_sem=recv_sem.at[t],
+                device_id={"chan": dst},
+                device_id_type=mesh_ids,
+            )
+        c.start()
+        copies.append((t, c))
+    for t, c in copies:
+        if t == 0:
+            c.wait()
+        else:
+            c.wait_send()
+    for t, c in copies:
+        if t != 0:
+            c.wait_recv()
+
+
+def _project_send(full, w, n_c, cid):
+    rows, _ = full.shape
+    cols = w.shape[1] // n_c
+    return pl.pallas_call(
+        _project_send_kernel,
+        out_shape=jax.ShapeDtypeStruct((n_c, rows, cols), full.dtype),
+        in_specs=[pl.BlockSpec(memory_space=pltpu.VMEM)] * 2,
+        out_specs=pl.BlockSpec(memory_space=pl.ANY),
+        scratch_shapes=[
+            pltpu.VMEM((n_c, rows, cols), full.dtype),
+            pltpu.SemaphoreType.DMA((n_c,)),
+            pltpu.SemaphoreType.DMA((n_c,)),
+        ],
+        compiler_params=pltpu.CompilerParams(collective_id=cid, has_side_effects=True),
+    )(full, w)
+
+
 def body(tokens, gate_in, mix_first, mix_second, twiddle, out_proj):
     seq_rows, chan_cols = tokens.shape
     n_seq = lax.axis_size("seq")
@@ -198,8 +252,7 @@
     full = _back_gate_send(mix_second, got, gate, n_seq, n_chan, CHUNKS, 1)
     rows_per = seq_rows // n_chan
     full = full.reshape(rows_per, n_chan * chan_cols)
-    mixed = jnp.dot(full, out_proj, preferred_element_type=jnp.float32).astype(jnp.bfloat16)
-    res = _a2a(mixed, "chan", 3, n=n_chan)
+    res = _project_send(full, out_proj, n_chan, 3)
     return res.reshape(seq_rows, chan_cols)
 
 

time: 227 us -> 237 us (1.044)
  the two profiles are of different devices: /device:TPU:119 before, /device:TPU:75 now
where the time goes in v14:
time: 237 us; the launch traced here: 236 us
  Pallas kernels  227 us (96%)
  local copies, waits for them, and re-layouts  5.48 us (2%)
  matrix products  3.5 us (1%)
    pallas_call x1, Pallas kernels, _back_gate_send(): pl.pallas_call(functools.partial(_back_gate_send_kernel, k_chunks), out_s...  139 us
    pallas_call x1, Pallas kernels, _a2a(): pl.pallas_call(functools.partial(_a2a_kernel, axis, n), out_shape=jax.Sha...  47.9 us
    pallas_call x1, Pallas kernels, _project_send(): pl.pallas_call(_project_send_kernel, out_shape=jax.ShapeDtypeStruct((n_c,...  40.6 us

profile of v14, /device:TPU:75, one launch (start us, length us, event | category | flops | bytes accessed | tf_op | source)
XLA Modules:
  0.0 236.3 jit_solution(8658700118736103282)
XLA Ops:
  0.0 0.0 copy-start
  0.0 1.6 copy-done
  1.6 0.8 reshape.24
  2.4 3.5 %fusion.x_ref = bf16[8,16,64,128]{3,2,1,0:T(8,128)(2,1)} fusion(bf16[16,512,128,1]{2,1,0,3:T(8,128)(2,1)S(1)} %bitcast.21, bf16[8,64,512,1]{2,1,3,0:T(8,128)(2,1)} %bitcast.27, f32[8,16,64]{2,1,0:T(8,128)S(1)} %bitcast.26), kind=kOutput, calls=%fused_computation.1 | convolution fusion | flops 1075838976 | bytes 4751360 | tf_op jit(solution)/shard_map/dik,bkc->dbic/dot_general | solution.py:247
  5.9 47.9 %shard_map.64 = bf16[8,16,64,128]{3,2,1,0:T(8,128)(2,1)} custom-call(bf16[8,16,64,128]{3,2,1,0:T(8,128)(2,1)} %fusion.x_ref), custom_call_target="tpu_custom_call" | custom-call | tf_op jit(solution)/shard_map/pallas_call | solution.py:57
  53.9 138.7 %shard_map.65 = bf16[2,8,64,1024]{3,2,1,0:T(8,128)(2,1)} custom-call(bf16[128,128]{1,0:T(8,128)(2,1)} %m_ref.1, bf16[128,64,128]{2,1,0:T(8,128)(2,1)} %bitcast.23, bf16[16,512,128]{2,1,0:T(8,128)(2,1)} %bitcast.25), custom_call_target="tpu_custom_call" | custom-call | tf_op jit(solution)/shard_map/pallas_call | solution.py:162
  192.6 40.6 %shard_map.66 = bf16[8,1024,128]{2,1,0:T(8,128)(2,1)} custom-call(bf16[1024,1024]{1,0:T(8,128)(2,1)} %bitcast.22, bf16[1024,1024]{1,0:T(8,128)(2,1)} %w_ref.1), custom_call_target="tpu_custom_call" | custom-call | tf_op jit(solution)/shard_map/pallas_call | solution.py:222
  233.2 3.0 %copy.14 = bf16[8192,128]{1,0:T(8,128)(2,1)} copy(bf16[8192,128]{1,0:T(8,128)(2,1)} %bitcast.24) | data formatting | bytes 4194304
  (1 shorter events, 0.0 us)
Async XLA Ops:
  0.0 1.6 copy-start

commit v15 on v7

--- a/solution.py
+++ b/solution.py
@@ -22,7 +22,7 @@
     local = pltpu.make_async_copy(x_ref.at[me], o_ref.at[me], loc_sem)
     local.start()
     copies = []
-    for t in range(1, n):
+    for t in list(range(1, n, 2)) + list(range(2, n, 2)):
         dst = (me + t) % n
         c = pltpu.make_async_remote_copy(
             src_ref=x_ref.at[dst],

time: 227 us -> 231 us (1.018)
  Pallas kernels: 210 us -> 215 us
    pallas_call x2, Pallas kernels: 93.9 us -> 98 us  [_a2a(): pl.pallas_call(functools.partial(_a2a_kernel, axis, n), out_shape=jax.Sha...]
where the time goes in v15:
time: 231 us; the launch traced here: 230 us
  Pallas kernels  215 us (93%)
  local copies, waits for them, and re-layouts  7.85 us (3%)
  matrix products  7.08 us (3%)
    pallas_call x1, Pallas kernels, _back_gate_send(): pl.pallas_call(functools.partial(_back_gate_send_kernel, k_chunks), out_s...  117 us
    pallas_call x2, Pallas kernels, _a2a(): pl.pallas_call(functools.partial(_a2a_kernel, axis, n), out_shape=jax.Sha...  98 us
    unnamed x6, local copies, waits for them, and re-layouts  7 us

profile of v15, /device:TPU:119, one launch (start us, length us, event | category | flops | bytes accessed | tf_op | source)
XLA Modules:
  0.0 230.2 jit_solution(7969228967842312447)
XLA Ops:
  0.0 0.0 copy-start
  0.0 1.6 copy-done
  1.6 0.8 reshape.27
  2.4 3.5 %fusion.x_ref = bf16[8,16,64,128]{3,2,1,0:T(8,128)(2,1)} fusion(bf16[16,512,128,1]{2,1,0,3:T(8,128)(2,1)S(1)} %bitcast.34, bf16[8,64,512,1]{2,1,3,0:T(8,128)(2,1)} %bitcast.42, f32[8,16,64]{2,1,0:T(8,128)S(1)} %bitcast.41), kind=kOutput, calls=%fused_computation.2 | convolution fusion | flops 1075838976 | bytes 4751360 | tf_op jit(solution)/shard_map/dik,bkc->dbic/dot_general | solution.py:182
  5.9 49.2 %shard_map.64 = bf16[8,16,64,128]{3,2,1,0:T(8,128)(2,1)} custom-call(bf16[8,16,64,128]{3,2,1,0:T(8,128)(2,1)} %fusion.x_ref), custom_call_target="tpu_custom_call" | custom-call | tf_op jit(solution)/shard_map/pallas_call | solution.py:46
  55.1 117.3 %shard_map.65 = bf16[8,2,8,64,128]{4,3,2,1,0:T(8,128)(2,1)} custom-call(bf16[128,128]{1,0:T(8,128)(2,1)} %m_ref.1, bf16[128,64,128]{2,1,0:T(8,128)(2,1)} %bitcast.35, bf16[16,512,128]{2,1,0:T(8,128)(2,1)} %bitcast.37), custom_call_target="tpu_custom_call" | custom-call | tf_op jit(solution)/shard_map/pallas_call | solution.py:151
  172.4 0.0 copy-start.1
  172.4 2.4 %copy.13 = bf16[128,8,8,128]{3,2,1,0:T(8,128)(2,1)S(1)} copy(bf16[128,8,8,128]{3,1,2,0:T(8,128)(2,1)} %bitcast.39) | data formatting | bytes 4194304
  174.8 0.0 copy-done.1
  174.8 3.6 %fusion.2.x_ref = bf16[8,1024,128]{2,1,0:T(8,128)(2,1)} fusion(bf16[8,1024,128,1]{2,1,0,3:T(8,128)(2,1)S(1)} %bitcast.38, bf16[8,128,8,128]{3,2,1,0:T(8,128)(2,1)S(1)} %bitcast.40), kind=kOutput, calls=%fused_computation.4 | convolution fusion | flops 2148532224 | bytes 6291456 | tf_op jit(solution)/shard_map/spc,scex->epx/dot_general | solution.py:191
  178.4 48.8 %shard_map.66 = bf16[8,1024,128]{2,1,0:T(8,128)(2,1)} custom-call(bf16[8,1024,128]{2,1,0:T(8,128)(2,1)} %fusion.2.x_ref), custom_call_target="tpu_custom_call" | custom-call | tf_op jit(solution)/shard_map/pallas_call | solution.py:46
  227.2 3.0 %copy.21 = bf16[8192,128]{1,0:T(8,128)(2,1)} copy(bf16[8192,128]{1,0:T(8,128)(2,1)} %bitcast.36) | data formatting | bytes 4194304
  (1 shorter events, 0.0 us)
Async XLA Ops:
  0.0 1.6 copy-start
  172.4 2.4 %copy-start.1 = (bf16[8,2,8,64,128]{4,3,2,1,0:T(8,128)(2,1)S(1)}, bf16[8,2,8,64,128]{4,3,2,1,0:T(8,128)(2,1)}, u32[]{:S(2)}) copy-start(bf16[8,2,8,64,128]{4,3,2,1,0:T(8,128)(2,1)} %shard_map.65) | copy-start | bytes 6291460

commit v16 on v12

--- a/solution.py
+++ b/solution.py
@@ -8,7 +8,7 @@
 from jax.experimental.pallas import tpu as pltpu
 
 B1 = 512
-CHUNKS = 4
+CHUNKS = 2
 LEAD = 1
 
 

time: 229 us -> 229 us (level)
  the two profiles are of different devices: /device:TPU:119 before, /device:TPU:49 now
where the time goes in v16:
time: 229 us
  Pallas kernels  214 us (93%)
  local copies, waits for them, and re-layouts  7.85 us (3%)
  matrix products  7.1 us (3%)
    pallas_call x1, Pallas kernels, _back_gate_send(): pl.pallas_call(functools.partial(_back_gate_send_kernel, k_chunks), out_s...  120 us
    pallas_call x2, Pallas kernels, _a2a(): pl.pallas_call(functools.partial(_a2a_kernel, axis, n), out_shape=jax.Sha...  94.5 us
    unnamed x6, local copies, waits for them, and re-layouts  7 us

profile of v16, /device:TPU:49, one launch (start us, length us, event | category | flops | bytes accessed | tf_op | source)
XLA Modules:
  0.0 229.1 jit_solution(10453659961833563723)
XLA Ops:
  0.0 0.0 copy-start
  0.0 1.6 copy-done
  1.6 0.8 reshape.27
  2.4 3.5 %fusion.x_ref = bf16[8,16,64,128]{3,2,1,0:T(8,128)(2,1)} fusion(bf16[16,512,128,1]{2,1,0,3:T(8,128)(2,1)S(1)} %bitcast.34, bf16[8,64,512,1]{2,1,3,0:T(8,128)(2,1)} %bitcast.42, f32[8,16,64]{2,1,0:T(8,128)S(1)} %bitcast.41), kind=kOutput, calls=%fused_computation.2 | convolution fusion | flops 1075838976 | bytes 4751360 | tf_op jit(solution)/shard_map/dik,bkc->dbic/dot_general | solution.py:182
  6.0 50.1 %shard_map.64 = bf16[8,16,64,128]{3,2,1,0:T(8,128)(2,1)} custom-call(bf16[8,16,64,128]{3,2,1,0:T(8,128)(2,1)} %fusion.x_ref), custom_call_target="tpu_custom_call" | custom-call | tf_op jit(solution)/shard_map/pallas_call | solution.py:46
  56.0 119.7 %shard_map.65 = bf16[8,2,8,64,128]{4,3,2,1,0:T(8,128)(2,1)} custom-call(bf16[128,128]{1,0:T(8,128)(2,1)} %m_ref.1, bf16[128,64,128]{2,1,0:T(8,128)(2,1)} %bitcast.35, bf16[16,512,128]{2,1,0:T(8,128)(2,1)} %bitcast.37), custom_call_target="tpu_custom_call" | custom-call | tf_op jit(solution)/shard_map/pallas_call | solution.py:151
  175.7 0.0 copy-start.1
  175.7 2.4 %copy.13 = bf16[128,8,8,128]{3,2,1,0:T(8,128)(2,1)S(1)} copy(bf16[128,8,8,128]{3,1,2,0:T(8,128)(2,1)} %bitcast.39) | data formatting | bytes 4194304
  178.1 0.0 copy-done.1
  178.1 3.6 %fusion.2.x_ref = bf16[8,1024,128]{2,1,0:T(8,128)(2,1)} fusion(bf16[8,1024,128,1]{2,1,0,3:T(8,128)(2,1)S(1)} %bitcast.38, bf16[8,128,8,128]{3,2,1,0:T(8,128)(2,1)S(1)} %bitcast.40), kind=kOutput, calls=%fused_computation.4 | convolution fusion | flops 2148532224 | bytes 6291456 | tf_op jit(solution)/shard_map/spc,scex->epx/dot_general | solution.py:191
  181.7 44.4 %shard_map.66 = bf16[8,1024,128]{2,1,0:T(8,128)(2,1)} custom-call(bf16[8,1024,128]{2,1,0:T(8,128)(2,1)} %fusion.2.x_ref), custom_call_target="tpu_custom_call" | custom-call | tf_op jit(solution)/shard_map/pallas_call | solution.py:46
  226.1 3.0 %copy.21 = bf16[8192,128]{1,0:T(8,128)(2,1)} copy(bf16[8192,128]{1,0:T(8,128)(2,1)} %bitcast.36) | data formatting | bytes 4194304
  (1 shorter events, 0.0 us)
Async XLA Ops:
  0.0 1.6 copy-start
  175.7 2.4 %copy-start.1 = (bf16[8,2,8,64,128]{4,3,2,1,0:T(8,128)(2,1)S(1)}, bf16[8,2,8,64,128]{4,3,2,1,0:T(8,128)(2,1)}, u32[]{:S(2)}) copy-start(bf16[8,2,8,64,128]{4,3,2,1,0:T(8,128)(2,1)} %shard_map.65) | copy-start | bytes 6291460

commit v17 on v9

--- a/solution.py
+++ b/solution.py
@@ -175,36 +175,33 @@
     barrier = pltpu.get_barrier_semaphore()
     for t in range(1, n):
         pl.semaphore_signal(barrier, inc=1, device_id={"seq": (me + t) % n}, device_id_type=mesh_ids)
-    pl.semaphore_wait(barrier, n - 1)
-    copies = []
-    for t in list(range(1, n)) + [0]:
-        dst = (me + t) % n
-        rows = pl.ds(pl.multiple_of(dst * n_i, n_i), n_i)
+    for d in range(n):
+        rows = pl.ds(d * n_i, n_i)
         m = mf_ref[rows, :]
         for b in range(n_b):
             part = jnp.dot(m, tok_ref[b], preferred_element_type=jnp.float32)
-            stage[t, b] = (part * tw_ref[rows, pl.ds(b, 1)]).astype(stage.dtype)
-        if t == 0:
-            c = pltpu.make_async_copy(stage.at[t], got_ref.at[me], recv_sem.at[0])
-        else:
-            c = pltpu.make_async_remote_copy(
-                src_ref=stage.at[t],
-                dst_ref=got_ref.at[me],
-                send_sem=send_sem.at[t],
-                recv_sem=recv_sem.at[t],
-                device_id={"seq": dst},
-                device_id_type=mesh_ids,
-            )
+            stage[d, b] = (part * tw_ref[rows, pl.ds(b, 1)]).astype(stage.dtype)
+    pl.semaphore_wait(barrier, n - 1)
+    local = pltpu.make_async_copy(stage.at[me], got_ref.at[me], recv_sem.at[0])
+    local.start()
+    copies = []
+    for t in range(1, n):
+        dst = (me + t) % n
+        c = pltpu.make_async_remote_copy(
+            src_ref=stage.at[dst],
+            dst_ref=got_ref.at[me],
+            send_sem=send_sem.at[t],
+            recv_sem=recv_sem.at[t],
+            device_id={"seq": dst},
+            device_id_type=mesh_ids,
+        )
         c.start()
-        copies.append((t, c))
-    for t, c in copies:
-        if t == 0:
-            c.wait()
-        else:
-            c.wait_send()
-    for t, c in copies:
-        if t != 0:
-            c.wait_recv()
+        copies.append(c)
+    local.wait()
+    for c in copies:
+        c.wait_send()
+    for c in copies:
+        c.wait_recv()
 
 
 def _first_send(mix_first, blocked, tw_t, n, cid):

time: 230 us -> 229 us (level)
  no operation moved by 1% of the time
where the time goes in v17:
time: 229 us
  Pallas kernels  219 us (96%)
  local copies, waits for them, and re-layouts  6.22 us (3%)
  matrix products  3.57 us (2%)
    pallas_call x1, Pallas kernels, _back_gate_send(): pl.pallas_call(functools.partial(_back_gate_send_kernel, k_chunks), out_s...  120 us
    pallas_call x1, Pallas kernels, _first_send(): pl.pallas_call(_first_send_kernel, out_shape=jax.ShapeDtypeStruct((n, n_b...  50.8 us
    pallas_call x1, Pallas kernels, _a2a(): pl.pallas_call(functools.partial(_a2a_kernel, axis, n), out_shape=jax.Sha...  48.6 us
    unnamed x7, local copies, waits for them, and re-layouts  6.22 us

profile of v17, /device:TPU:119, one launch (start us, length us, event | category | flops | bytes accessed | tf_op | source)
XLA Modules:
  0.0 228.9 jit_solution(8836086488392934403)
XLA Ops:
  0.0 1.6 copy.7
  1.6 50.8 %shard_map.64 = bf16[8,16,64,128]{3,2,1,0:T(8,128)(2,1)} custom-call(bf16[512,512]{1,0:T(8,128)(2,1)} %mf_ref.1, bf16[16,512,128]{2,1,0:T(8,128)(2,1)} %bitcast.23, f32[512,16]{1,0:T(8,128)} %bitcast.26), custom_call_target="tpu_custom_call" | custom-call | tf_op jit(solution)/shard_map/pallas_call | solution.py:210
  52.4 0.0 copy-start.1
  52.5 119.6 %shard_map.65 = bf16[8,2,8,64,128]{4,3,2,1,0:T(8,128)(2,1)} custom-call(bf16[128,128]{1,0:T(8,128)(2,1)} %m_ref.1, bf16[128,64,128]{2,1,0:T(8,128)(2,1)} %bitcast.19, bf16[16,512,128]{2,1,0:T(8,128)(2,1)} %bitcast.21), custom_call_target="tpu_custom_call" | custom-call | tf_op jit(solution)/shard_map/pallas_call | solution.py:151
  172.1 0.0 copy-done.1
  172.1 0.0 copy-start
  172.1 0.6 copy.10
  172.7 0.9 copy-done
  173.7 3.6 %fusion.1.x_ref = bf16[8,1024,128]{2,1,0:T(8,128)(2,1)} fusion(bf16[8,1024,128,1]{2,1,0,3:T(8,128)(2,1)S(1)} %bitcast.22, bf16[8,128,8,128]{3,2,1,0:T(8,128)(2,1)S(1)} %bitcast.25), kind=kOutput, calls=%fused_computation.2 | convolution fusion | flops 2148532224 | bytes 6291456 | tf_op jit(solution)/shard_map/spc,scex->epx/dot_general | solution.py:240
  177.3 48.6 %shard_map.66 = bf16[8,1024,128]{2,1,0:T(8,128)(2,1)} custom-call(bf16[8,1024,128]{2,1,0:T(8,128)(2,1)} %fusion.1.x_ref), custom_call_target="tpu_custom_call" | custom-call | tf_op jit(solution)/shard_map/pallas_call | solution.py:46
  225.9 3.0 %copy.16 = bf16[8192,128]{1,0:T(8,128)(2,1)} copy(bf16[8192,128]{1,0:T(8,128)(2,1)} %bitcast.20) | data formatting | bytes 4194304
Async XLA Ops:
  52.4 119.7 %copy-start.1 = (bf16[1024,1024]{1,0:T(8,128)(2,1)S(1)}, bf16[1024,1024]{1,0:T(8,128)(2,1)}, u32[]{:S(2)}) copy-start(bf16[1024,1024]{1,0:T(8,128)(2,1)} %param.11) | copy-start | bytes 6291460
  172.1 1.6 copy-start

commit v18 on v7

--- a/solution.py
+++ b/solution.py
@@ -57,8 +57,8 @@
     )(x)
 
 
-def _back_gate_send_kernel(k_chunks, m_ref, got_ref, gate_ref, full_ref, sec, recv_s, gv, hid,
-                           s_send, s_recv, c_send, c_recv, g_sem):
+def _back_gate_send_kernel(k_chunks, m_ref, got_ref, gate_ref, full_ref, sec, recv_s, hid,
+                           s_send, s_recv, c_send, c_recv):
     n_s, n_j, n_i, _ = sec.shape
     n_c = full_ref.shape[0]
     jp = n_j // n_c
@@ -73,8 +73,6 @@
         pl.semaphore_signal(barrier, inc=1, device_id={"chan": (me_c + t) % n_c}, device_id_type=mesh_ids)
     pl.semaphore_wait(barrier, (n_s - 1) + (n_c - 1))
 
-    gcopy = pltpu.make_async_copy(gate_ref, gv, g_sem)
-    gcopy.start()
     def issue_seq(k):
         isl = pl.ds(k * w, w)
         m = m_ref[...]
@@ -100,7 +98,6 @@
         return row
 
     seq_copies = [issue_seq(k) for k in range(min(LEAD, k_chunks))]
-    gcopy.wait()
     chan_copies = []
     for k in range(k_chunks):
         isl = pl.ds(k * w, w)
@@ -110,7 +107,7 @@
             else:
                 seq_copies[k][t].wait_recv()
         for s in range(n_s):
-            prod = recv_s[s, :, isl, :].astype(jnp.float32) * gv[:, pl.ds(s * n_i + k * w, w), :].astype(jnp.float32)
+            prod = recv_s[s, :, isl, :].astype(jnp.float32) * gate_ref[:, pl.ds(s * n_i + k * w, w), :].astype(jnp.float32)
             hid[:, s, isl, :] = prod.astype(hid.dtype)
         for t in range(n_c):
             dst = (me_c + t) % n_c
@@ -151,18 +148,16 @@
     return pl.pallas_call(
         functools.partial(_back_gate_send_kernel, k_chunks),
         out_shape=jax.ShapeDtypeStruct((n_c, jp, n_s, n_i, cols), got.dtype),
-        in_specs=[pl.BlockSpec(memory_space=pltpu.VMEM)] * 2 + [pl.BlockSpec(memory_space=pl.ANY)],
+        in_specs=[pl.BlockSpec(memory_space=pltpu.VMEM)] * 3,
         out_specs=pl.BlockSpec(memory_space=pl.ANY),
         scratch_shapes=[
             pltpu.VMEM((n_s, n_j, n_i, cols), got.dtype),
             pltpu.VMEM((n_s, n_j, n_i, cols), got.dtype),
-            pltpu.VMEM((n_j, n_s * n_i, cols), got.dtype),
             pltpu.VMEM((n_j, n_s, n_i, cols), got.dtype),
             pltpu.SemaphoreType.DMA((k_chunks, n_s)),
             pltpu.SemaphoreType.DMA((k_chunks, n_s)),
             pltpu.SemaphoreType.DMA((k_chunks, n_c)),
             pltpu.SemaphoreType.DMA((k_chunks, n_c)),
-            pltpu.SemaphoreType.DMA,
         ],
         compiler_params=pltpu.CompilerParams(collective_id=cid, has_side_effects=True),
     )(m2, got, gate)

time: 227 us -> 227 us (level)
  no operation moved by 1% of the time
where the time goes in v18:
time: 227 us; the launch traced here: 226 us
  Pallas kernels  211 us (93%)
  local copies, waits for them, and re-layouts  7.85 us (3%)
  matrix products  7.08 us (3%)
    pallas_call x1, Pallas kernels, _back_gate_send(): pl.pallas_call(functools.partial(_back_gate_send_kernel, k_chunks), out_s...  117 us
    pallas_call x2, Pallas kernels, _a2a(): pl.pallas_call(functools.partial(_a2a_kernel, axis, n), out_shape=jax.Sha...  93.9 us
    unnamed x6, local copies, waits for them, and re-layouts  7 us

profile of v18, /device:TPU:119, one launch (start us, length us, event | category | flops | bytes accessed | tf_op | source)
XLA Modules:
  0.0 225.7 jit_solution(16079380607765882501)
XLA Ops:
  0.0 0.0 copy-start
  0.0 1.6 copy-done
  1.6 0.8 reshape.27
  2.4 3.5 %fusion.x_ref = bf16[8,16,64,128]{3,2,1,0:T(8,128)(2,1)} fusion(bf16[16,512,128,1]{2,1,0,3:T(8,128)(2,1)S(1)} %bitcast.34, bf16[8,64,512,1]{2,1,3,0:T(8,128)(2,1)} %bitcast.42, f32[8,16,64]{2,1,0:T(8,128)S(1)} %bitcast.41), kind=kOutput, calls=%fused_computation.2 | convolution fusion | flops 1075838976 | bytes 4751360 | tf_op jit(solution)/shard_map/dik,bkc->dbic/dot_general | solution.py:177
  5.9 49.3 %shard_map.64 = bf16[8,16,64,128]{3,2,1,0:T(8,128)(2,1)} custom-call(bf16[8,16,64,128]{3,2,1,0:T(8,128)(2,1)} %fusion.x_ref), custom_call_target="tpu_custom_call" | custom-call | tf_op jit(solution)/shard_map/pallas_call | solution.py:46
  55.3 116.8 %shard_map.65 = bf16[8,2,8,64,128]{4,3,2,1,0:T(8,128)(2,1)} custom-call(bf16[128,128]{1,0:T(8,128)(2,1)} %m_ref.1, bf16[128,64,128]{2,1,0:T(8,128)(2,1)} %bitcast.35, bf16[16,512,128]{2,1,0:T(8,128)(2,1)} %bitcast.37), custom_call_target="tpu_custom_call" | custom-call | tf_op jit(solution)/shard_map/pallas_call | solution.py:148
  172.1 0.0 copy-start.1
  172.1 2.4 %copy.13 = bf16[128,8,8,128]{3,2,1,0:T(8,128)(2,1)S(1)} copy(bf16[128,8,8,128]{3,1,2,0:T(8,128)(2,1)} %bitcast.39) | data formatting | bytes 4194304
  174.5 0.0 copy-done.1
  174.5 3.6 %fusion.2.x_ref = bf16[8,1024,128]{2,1,0:T(8,128)(2,1)} fusion(bf16[8,1024,128,1]{2,1,0,3:T(8,128)(2,1)S(1)} %bitcast.38, bf16[8,128,8,128]{3,2,1,0:T(8,128)(2,1)S(1)} %bitcast.40), kind=kOutput, calls=%fused_computation.4 | convolution fusion | flops 2148532224 | bytes 6291456 | tf_op jit(solution)/shard_map/spc,scex->epx/dot_general | solution.py:186
  178.1 44.6 %shard_map.66 = bf16[8,1024,128]{2,1,0:T(8,128)(2,1)} custom-call(bf16[8,1024,128]{2,1,0:T(8,128)(2,1)} %fusion.2.x_ref), custom_call_target="tpu_custom_call" | custom-call | tf_op jit(solution)/shard_map/pallas_call | solution.py:46
  222.7 3.0 %copy.21 = bf16[8192,128]{1,0:T(8,128)(2,1)} copy(bf16[8192,128]{1,0:T(8,128)(2,1)} %bitcast.36) | data formatting | bytes 4194304
  (1 shorter events, 0.0 us)
Async XLA Ops:
  0.0 1.6 copy-start
  172.1 2.4 %copy-start.1 = (bf16[8,2,8,64,128]{4,3,2,1,0:T(8,128)(2,1)S(1)}, bf16[8,2,8,64,128]{4,3,2,1,0:T(8,128)(2,1)}, u32[]{:S(2)}) copy-start(bf16[8,2,8,64,128]{4,3,2,1,0:T(8,128)(2,1)} %shard_map.65) | copy-start | bytes 6291460

commit v19 on v7

--- a/solution.py
+++ b/solution.py
@@ -190,7 +190,7 @@
     wts = out_proj.reshape(n_chan, chan_cols, n_chan, d_out // n_chan)
     mixed = jnp.einsum("spc,scex->epx", full, wts, preferred_element_type=jnp.float32)
     mixed = mixed.astype(jnp.bfloat16)
-    res = _a2a(mixed, "chan", 3)
+    res = lax.all_to_all(mixed, "chan", split_axis=0, concat_axis=0, tiled=False)
     return res.reshape(seq_rows, chan_cols)
 
 

time: 227 us -> 229 us (level)
  blocking collectives: 0 us -> 46.4 us
  Pallas kernels: 210 us -> 165 us
    all_to_all x0 -> x1, blocking collectives: none -> 46.4 us  [body(): lax.all_to_all(mixed, 'chan', split_axis=0, concat_axis=0, tiled=False)]
    pallas_call x2 -> x1, Pallas kernels: 93.9 us -> 49.3 us  [_a2a(): pl.pallas_call(functools.partial(_a2a_kernel, axis, n), out_shape=jax.Sha...]
    unnamed x6 -> x4, local copies, waits for them, and re-layouts: 7 us -> 5.47 us
where the time goes in v19:
time: 229 us; the launch traced here: 226 us
  Pallas kernels  165 us (72%)
  blocking collectives  46.4 us (20%)
  matrix products  8.03 us (4%)
  local copies, waits for them, and re-layouts  6.47 us (3%)
    pallas_call x1, Pallas kernels, _back_gate_send(): pl.pallas_call(functools.partial(_back_gate_send_kernel, k_chunks), out_s...  116 us
    pallas_call x1, Pallas kernels, _a2a(): pl.pallas_call(functools.partial(_a2a_kernel, axis, n), out_shape=jax.Sha...  49.3 us
    all_to_all x1, blocking collectives, body(): lax.all_to_all(mixed, 'chan', split_axis=0, concat_axis=0, tiled=False)  46.4 us
    unnamed x4, local copies, waits for them, and re-layouts  5.47 us

profile of v19, /device:TPU:119, one launch (start us, length us, event | category | flops | bytes accessed | tf_op | source)
XLA Modules:
  0.0 226.3 jit_solution(17423018454126746493)
XLA Ops:
  0.0 0.0 copy-start
  0.0 1.0 reshape.27
  1.0 0.6 copy-done
  1.6 3.5 %fusion.x_ref = bf16[8,16,64,128]{3,2,1,0:T(8,128)(2,1)} fusion(bf16[16,512,128,1]{2,1,0,3:T(8,128)(2,1)S(1)} %bitcast.34, bf16[8,64,512,1]{2,1,3,0:T(8,128)(2,1)} %bitcast.42, f32[8,16,64]{2,1,0:T(8,128)S(1)} %bitcast.41), kind=kOutput, calls=%fused_computation.2 | convolution fusion | flops 1075838976 | bytes 4751360 | tf_op jit(solution)/shard_map/dik,bkc->dbic/dot_general | solution.py:182
  5.1 49.3 %shard_map.64 = bf16[8,16,64,128]{3,2,1,0:T(8,128)(2,1)} custom-call(bf16[8,16,64,128]{3,2,1,0:T(8,128)(2,1)} %fusion.x_ref), custom_call_target="tpu_custom_call" | custom-call | tf_op jit(solution)/shard_map/pallas_call | solution.py:46
  54.4 3.5 %copy.13 = bf16[128,8,8,128]{3,2,1,0:T(8,128)(2,1)} copy(bf16[128,8,8,128]{3,1,2,0:T(8,128)(2,1)} %bitcast.39) | data formatting | bytes 4194304
  58.0 116.0 %shard_map.65 = bf16[8,2,8,64,128]{4,3,2,1,0:T(8,128)(2,1)} custom-call(bf16[128,128]{1,0:T(8,128)(2,1)} %m_ref.1, bf16[128,64,128]{2,1,0:T(8,128)(2,1)} %bitcast.35, bf16[16,512,128]{2,1,0:T(8,128)(2,1)} %bitcast.37), custom_call_target="tpu_custom_call" | custom-call | tf_op jit(solution)/shard_map/pallas_call | solution.py:151
  174.0 4.6 %fusion.2 = bf16[8,1024,128]{2,1,0:T(8,128)(2,1)S(1)} fusion(bf16[8,1024,128,1]{2,1,0,3:T(8,128)(2,1)} %bitcast.38, bf16[8,128,8,128]{3,2,1,0:T(8,128)(2,1)} %bitcast.40), kind=kOutput, calls=%fused_computation.4 | convolution fusion | flops 2148532224 | bytes 6291456 | tf_op jit(solution)/shard_map/spc,scex->epx/dot_general | solution.py:191
  178.6 46.4 %all_to_all.5 = bf16[8,1024,128]{2,1,0:T(8,128)(2,1)S(1)} all-to-all(bf16[8,1024,128]{2,1,0:T(8,128)(2,1)S(1)} %fusion.2), channel_id=1, replica_groups=mesh['seq'=8,'chan'=8,'batch'=4] {'chan'}, dimensions={0} | all-to-all | bytes 4194304 | tf_op jit(solution)/shard_map/all_to_all | solution.py:193
  225.0 1.3 copy.21
  (1 shorter events, 0.0 us)
Async XLA Ops:
  0.0 1.6 copy-start

commit v20 on v7

--- a/solution.py
+++ b/solution.py
@@ -71,16 +71,20 @@
         pl.semaphore_signal(barrier, inc=1, device_id={"seq": (me_s + t) % n_s}, device_id_type=mesh_ids)
     for t in range(1, n_c):
         pl.semaphore_signal(barrier, inc=1, device_id={"chan": (me_c + t) % n_c}, device_id_type=mesh_ids)
-    pl.semaphore_wait(barrier, (n_s - 1) + (n_c - 1))
 
     gcopy = pltpu.make_async_copy(gate_ref, gv, g_sem)
     gcopy.start()
-    def issue_seq(k):
-        isl = pl.ds(k * w, w)
+
+    def compute_sec(k):
         m = m_ref[...]
         for i in range(k * w, (k + 1) * w):
             part = jnp.dot(m, got_ref[:, i, :], preferred_element_type=jnp.float32)
             sec[:, :, i, :] = part.astype(sec.dtype).reshape(n_s, n_j, part.shape[-1])
+
+    def issue_seq(k, computed=False):
+        isl = pl.ds(k * w, w)
+        if not computed:
+            compute_sec(k)
         row = []
         for t in range(n_s):
             if t == 0:
@@ -99,7 +103,10 @@
             row.append(c)
         return row
 
-    seq_copies = [issue_seq(k) for k in range(min(LEAD, k_chunks))]
+    for k in range(min(LEAD, k_chunks)):
+        compute_sec(k)
+    pl.semaphore_wait(barrier, (n_s - 1) + (n_c - 1))
+    seq_copies = [issue_seq(k, computed=True) for k in range(min(LEAD, k_chunks))]
     gcopy.wait()
     chan_copies = []
     for k in range(k_chunks):

time: 227 us -> 220 us (0.969)
  Pallas kernels: 210 us -> 203 us
    pallas_call x1, Pallas kernels: 116 us -> 107 us  [_back_gate_send(): pl.pallas_call(functools.partial(_back_gate_send_kernel, k_chunks), out_s...]
where the time goes in v20:
time: 220 us; the launch traced here: 218 us
  Pallas kernels  203 us (92%)
  local copies, waits for them, and re-layouts  7.85 us (4%)
  matrix products  7.08 us (3%)
    pallas_call x1, Pallas kernels, _back_gate_send(): pl.pallas_call(functools.partial(_back_gate_send_kernel, k_chunks), out_s...  107 us
    pallas_call x2, Pallas kernels, _a2a(): pl.pallas_call(functools.partial(_a2a_kernel, axis, n), out_shape=jax.Sha...  95.7 us
    unnamed x6, local copies, waits for them, and re-layouts  7 us

profile of v20, /device:TPU:119, one launch (start us, length us, event | category | flops | bytes accessed | tf_op | source)
XLA Modules:
  0.0 217.8 jit_solution(18274213322311831585)
XLA Ops:
  0.0 0.0 copy-start
  0.0 1.6 copy-done
  1.6 0.8 reshape.27
  2.4 3.5 %fusion.x_ref = bf16[8,16,64,128]{3,2,1,0:T(8,128)(2,1)} fusion(bf16[16,512,128,1]{2,1,0,3:T(8,128)(2,1)S(1)} %bitcast.34, bf16[8,64,512,1]{2,1,3,0:T(8,128)(2,1)} %bitcast.42, f32[8,16,64]{2,1,0:T(8,128)S(1)} %bitcast.41), kind=kOutput, calls=%fused_computation.2 | convolution fusion | flops 1075838976 | bytes 4751360 | tf_op jit(solution)/shard_map/dik,bkc->dbic/dot_general | solution.py:189
  5.9 49.3 %shard_map.64 = bf16[8,16,64,128]{3,2,1,0:T(8,128)(2,1)} custom-call(bf16[8,16,64,128]{3,2,1,0:T(8,128)(2,1)} %fusion.x_ref), custom_call_target="tpu_custom_call" | custom-call | tf_op jit(solution)/shard_map/pallas_call | solution.py:46
  55.3 107.2 %shard_map.65 = bf16[8,2,8,64,128]{4,3,2,1,0:T(8,128)(2,1)} custom-call(bf16[128,128]{1,0:T(8,128)(2,1)} %m_ref.1, bf16[128,64,128]{2,1,0:T(8,128)(2,1)} %bitcast.35, bf16[16,512,128]{2,1,0:T(8,128)(2,1)} %bitcast.37), custom_call_target="tpu_custom_call" | custom-call | tf_op jit(solution)/shard_map/pallas_call | solution.py:158
  162.5 0.0 copy-start.1
  162.5 2.4 %copy.13 = bf16[128,8,8,128]{3,2,1,0:T(8,128)(2,1)S(1)} copy(bf16[128,8,8,128]{3,1,2,0:T(8,128)(2,1)} %bitcast.39) | data formatting | bytes 4194304
  164.8 0.0 copy-done.1
  164.8 3.6 %fusion.2.x_ref = bf16[8,1024,128]{2,1,0:T(8,128)(2,1)} fusion(bf16[8,1024,128,1]{2,1,0,3:T(8,128)(2,1)S(1)} %bitcast.38, bf16[8,128,8,128]{3,2,1,0:T(8,128)(2,1)S(1)} %bitcast.40), kind=kOutput, calls=%fused_computation.4 | convolution fusion | flops 2148532224 | bytes 6291456 | tf_op jit(solution)/shard_map/spc,scex->epx/dot_general | solution.py:198
  168.4 46.3 %shard_map.66 = bf16[8,1024,128]{2,1,0:T(8,128)(2,1)} custom-call(bf16[8,1024,128]{2,1,0:T(8,128)(2,1)} %fusion.2.x_ref), custom_call_target="tpu_custom_call" | custom-call | tf_op jit(solution)/shard_map/pallas_call | solution.py:46
  214.8 3.0 %copy.21 = bf16[8192,128]{1,0:T(8,128)(2,1)} copy(bf16[8192,128]{1,0:T(8,128)(2,1)} %bitcast.36) | data formatting | bytes 4194304
  (1 shorter events, 0.0 us)
Async XLA Ops:
  0.0 1.6 copy-start
  162.5 2.4 %copy-start.1 = (bf16[8,2,8,64,128]{4,3,2,1,0:T(8,128)(2,1)S(1)}, bf16[8,2,8,64,128]{4,3,2,1,0:T(8,128)(2,1)}, u32[]{:S(2)}) copy-start(bf16[8,2,8,64,128]{4,3,2,1,0:T(8,128)(2,1)} %shard_map.65) | copy-start | bytes 6291460

commit v21 on v20

--- a/solution.py
+++ b/solution.py
@@ -103,7 +103,7 @@
             row.append(c)
         return row
 
-    for k in range(min(LEAD, k_chunks)):
+    for k in range(k_chunks):
         compute_sec(k)
     pl.semaphore_wait(barrier, (n_s - 1) + (n_c - 1))
     seq_copies = [issue_seq(k, computed=True) for k in range(min(LEAD, k_chunks))]
@@ -137,7 +137,7 @@
             c.start()
             chan_copies.append((t, c))
         if k + LEAD < k_chunks:
-            seq_copies.append(issue_seq(k + LEAD))
+            seq_copies.append(issue_seq(k + LEAD, computed=True))
     for row in seq_copies:
         for c in row[1:]:
             c.wait_send()

time: 220 us -> 227 us (1.032)
  Pallas kernels: 203 us -> 209 us
    pallas_call x2, Pallas kernels: 95.7 us -> 102 us  [_a2a(): pl.pallas_call(functools.partial(_a2a_kernel, axis, n), out_shape=jax.Sha...]
where the time goes in v21:
time: 227 us; the launch traced here: 224 us
  Pallas kernels  209 us (92%)
  local copies, waits for them, and re-layouts  7.85 us (3%)
  matrix products  7.08 us (3%)
    pallas_call x1, Pallas kernels, _back_gate_send(): pl.pallas_call(functools.partial(_back_gate_send_kernel, k_chunks), out_s...  108 us
    pallas_call x2, Pallas kernels, _a2a(): pl.pallas_call(functools.partial(_a2a_kernel, axis, n), out_shape=jax.Sha...  102 us
    unnamed x6, local copies, waits for them, and re-layouts  7 us

profile of v21, /device:TPU:119, one launch (start us, length us, event | category | flops | bytes accessed | tf_op | source)
XLA Modules:
  0.0 224.0 jit_solution(9876624879300260658)
XLA Ops:
  0.0 0.0 copy-start
  0.0 1.6 copy-done
  1.6 0.8 reshape.27
  2.4 3.5 %fusion.x_ref = bf16[8,16,64,128]{3,2,1,0:T(8,128)(2,1)} fusion(bf16[16,512,128,1]{2,1,0,3:T(8,128)(2,1)S(1)} %bitcast.34, bf16[8,64,512,1]{2,1,3,0:T(8,128)(2,1)} %bitcast.42, f32[8,16,64]{2,1,0:T(8,128)S(1)} %bitcast.41), kind=kOutput, calls=%fused_computation.2 | convolution fusion | flops 1075838976 | bytes 4751360 | tf_op jit(solution)/shard_map/dik,bkc->dbic/dot_general | solution.py:189
  5.9 49.3 %shard_map.64 = bf16[8,16,64,128]{3,2,1,0:T(8,128)(2,1)} custom-call(bf16[8,16,64,128]{3,2,1,0:T(8,128)(2,1)} %fusion.x_ref), custom_call_target="tpu_custom_call" | custom-call | tf_op jit(solution)/shard_map/pallas_call | solution.py:46
  55.3 107.5 %shard_map.65 = bf16[8,2,8,64,128]{4,3,2,1,0:T(8,128)(2,1)} custom-call(bf16[128,128]{1,0:T(8,128)(2,1)} %m_ref.1, bf16[128,64,128]{2,1,0:T(8,128)(2,1)} %bitcast.35, bf16[16,512,128]{2,1,0:T(8,128)(2,1)} %bitcast.37), custom_call_target="tpu_custom_call" | custom-call | tf_op jit(solution)/shard_map/pallas_call | solution.py:158
  162.8 0.0 copy-start.1
  162.8 2.4 %copy.13 = bf16[128,8,8,128]{3,2,1,0:T(8,128)(2,1)S(1)} copy(bf16[128,8,8,128]{3,1,2,0:T(8,128)(2,1)} %bitcast.39) | data formatting | bytes 4194304
  165.2 0.0 copy-done.1
  165.2 3.6 %fusion.2.x_ref = bf16[8,1024,128]{2,1,0:T(8,128)(2,1)} fusion(bf16[8,1024,128,1]{2,1,0,3:T(8,128)(2,1)S(1)} %bitcast.38, bf16[8,128,8,128]{3,2,1,0:T(8,128)(2,1)S(1)} %bitcast.40), kind=kOutput, calls=%fused_computation.4 | convolution fusion | flops 2148532224 | bytes 6291456 | tf_op jit(solution)/shard_map/spc,scex->epx/dot_general | solution.py:198
  168.8 52.2 %shard_map.66 = bf16[8,1024,128]{2,1,0:T(8,128)(2,1)} custom-call(bf16[8,1024,128]{2,1,0:T(8,128)(2,1)} %fusion.2.x_ref), custom_call_target="tpu_custom_call" | custom-call | tf_op jit(solution)/shard_map/pallas_call | solution.py:46
  220.9 3.0 %copy.21 = bf16[8192,128]{1,0:T(8,128)(2,1)} copy(bf16[8192,128]{1,0:T(8,128)(2,1)} %bitcast.36) | data formatting | bytes 4194304
  (1 shorter events, 0.0 us)
Async XLA Ops:
  0.0 1.6 copy-start
  162.8 2.4 %copy-start.1 = (bf16[8,2,8,64,128]{4,3,2,1,0:T(8,128)(2,1)S(1)}, bf16[8,2,8,64,128]{4,3,2,1,0:T(8,128)(2,1)}, u32[]{:S(2)}) copy-start(bf16[8,2,8,64,128]{4,3,2,1,0:T(8,128)(2,1)} %shard_map.65) | copy-start | bytes 6291460

commit v22 on v20

--- a/solution.py
+++ b/solution.py
@@ -18,9 +18,9 @@
     for t in range(1, n):
         pl.semaphore_signal(barrier, inc=1, device_id={axis: (me + t) % n},
                             device_id_type=pl.DeviceIdType.MESH)
-    pl.semaphore_wait(barrier, n - 1)
     local = pltpu.make_async_copy(x_ref.at[me], o_ref.at[me], loc_sem)
     local.start()
+    pl.semaphore_wait(barrier, n - 1)
     copies = []
     for t in range(1, n):
         dst = (me + t) % n

time: 220 us -> 220 us (level)
  no operation moved by 1% of the time
where the time goes in v22:
time: 220 us; the launch traced here: 218 us
  Pallas kernels  203 us (92%)
  local copies, waits for them, and re-layouts  7.85 us (4%)
  matrix products  7.08 us (3%)
    pallas_call x1, Pallas kernels, _back_gate_send(): pl.pallas_call(functools.partial(_back_gate_send_kernel, k_chunks), out_s...  107 us
    pallas_call x2, Pallas kernels, _a2a(): pl.pallas_call(functools.partial(_a2a_kernel, axis, n), out_shape=jax.Sha...  95.7 us
    unnamed x6, local copies, waits for them, and re-layouts  7 us

profile of v22, /device:TPU:119, one launch (start us, length us, event | category | flops | bytes accessed | tf_op | source)
XLA Modules:
  0.0 217.8 jit_solution(3241821091089371531)
XLA Ops:
  0.0 0.0 copy-start
  0.0 1.6 copy-done
  1.6 0.8 reshape.27
  2.4 3.5 %fusion.x_ref = bf16[8,16,64,128]{3,2,1,0:T(8,128)(2,1)} fusion(bf16[16,512,128,1]{2,1,0,3:T(8,128)(2,1)S(1)} %bitcast.34, bf16[8,64,512,1]{2,1,3,0:T(8,128)(2,1)} %bitcast.42, f32[8,16,64]{2,1,0:T(8,128)S(1)} %bitcast.41), kind=kOutput, calls=%fused_computation.2 | convolution fusion | flops 1075838976 | bytes 4751360 | tf_op jit(solution)/shard_map/dik,bkc->dbic/dot_general | solution.py:189
  5.9 49.3 %shard_map.64 = bf16[8,16,64,128]{3,2,1,0:T(8,128)(2,1)} custom-call(bf16[8,16,64,128]{3,2,1,0:T(8,128)(2,1)} %fusion.x_ref), custom_call_target="tpu_custom_call" | custom-call | tf_op jit(solution)/shard_map/pallas_call | solution.py:46
  55.3 107.2 %shard_map.65 = bf16[8,2,8,64,128]{4,3,2,1,0:T(8,128)(2,1)} custom-call(bf16[128,128]{1,0:T(8,128)(2,1)} %m_ref.1, bf16[128,64,128]{2,1,0:T(8,128)(2,1)} %bitcast.35, bf16[16,512,128]{2,1,0:T(8,128)(2,1)} %bitcast.37), custom_call_target="tpu_custom_call" | custom-call | tf_op jit(solution)/shard_map/pallas_call | solution.py:158
  162.5 0.0 copy-start.1
  162.5 2.4 %copy.13 = bf16[128,8,8,128]{3,2,1,0:T(8,128)(2,1)S(1)} copy(bf16[128,8,8,128]{3,1,2,0:T(8,128)(2,1)} %bitcast.39) | data formatting | bytes 4194304
  164.8 0.0 copy-done.1
  164.8 3.6 %fusion.2.x_ref = bf16[8,1024,128]{2,1,0:T(8,128)(2,1)} fusion(bf16[8,1024,128,1]{2,1,0,3:T(8,128)(2,1)S(1)} %bitcast.38, bf16[8,128,8,128]{3,2,1,0:T(8,128)(2,1)S(1)} %bitcast.40), kind=kOutput, calls=%fused_computation.4 | convolution fusion | flops 2148532224 | bytes 6291456 | tf_op jit(solution)/shard_map/spc,scex->epx/dot_general | solution.py:198
  168.4 46.3 %shard_map.66 = bf16[8,1024,128]{2,1,0:T(8,128)(2,1)} custom-call(bf16[8,1024,128]{2,1,0:T(8,128)(2,1)} %fusion.2.x_ref), custom_call_target="tpu_custom_call" | custom-call | tf_op jit(solution)/shard_map/pallas_call | solution.py:46
  214.8 3.0 %copy.21 = bf16[8192,128]{1,0:T(8,128)(2,1)} copy(bf16[8192,128]{1,0:T(8,128)(2,1)} %bitcast.36) | data formatting | bytes 4194304
  (1 shorter events, 0.0 us)
Async XLA Ops:
  0.0 1.6 copy-start
  162.5 2.4 %copy-start.1 = (bf16[8,2,8,64,128]{4,3,2,1,0:T(8,128)(2,1)S(1)}, bf16[8,2,8,64,128]{4,3,2,1,0:T(8,128)(2,1)}, u32[]{:S(2)}) copy-start(bf16[8,2,8,64,128]{4,3,2,1,0:T(8,128)(2,1)} %shard_map.65) | copy-start | bytes 6291460
